TPU v7x, 32 devices: a whole 2x2x4 slice. The times are simulated.
32 devices in a mesh: groups: 2 (over x), seq: 16 (over z, y, core).
Axes of the slice: x: 2, y: 2, z: 4, core: 2. Of those that a mesh axis runs over, the one named last changes fastest.
Arguments:
- tokens: bfloat16 [4096, 1152], P(('groups', 'seq')), parts along dimension 0, may hold values from -30 to 30
- shift_cond: float32 [2304], P('groups'), parts along dimension 0, may hold values from -3 to 3
- scale_cond: float32 [2304], P('groups'), parts along dimension 0, may hold values from -3 to 3
- gate_cond: float32 [2304], P('groups'), parts along dimension 0, may hold values from -4 to 4
- qkv_weight: bfloat16 [1152, 3456], replicated, may hold values from -2 to 2
- out_weight: bfloat16 [1152, 1152], replicated, may hold values from -0.1875 to 0.1875
- cotangent: bfloat16 [4096, 1152], P(('groups', 'seq')), parts along dimension 0, may hold values from -6 to 6
Outputs:
- block_output: bfloat16 [4096, 1152], P(('groups', 'seq')), parts along dimension 0
- grad_input: bfloat16 [4096, 1152], P(('groups', 'seq')), parts along dimension 0
- grad_condition: float32 [6, 1152], P('groups'), parts along dimension 0
There are 2 independent parts, one for each index of `groups`. A program takes and returns all parts, laid end to end along the dimension named above; an argument that names none is the same for every part. Nothing has to cross between parts.
All inputs are finite; a program needn't handle non-finite values.
Results may differ from a plain program's by a relative error of at most 0.012.
The roundings to bfloat16 on the way count: a program that leaves them out, or rounds other values in their place, can miss the bound.
Values may be sent and summed in bfloat16 or wider, within the bound.
No kernel may reach another device: no remote copies, remote signals or barrier semaphores. Data moves between devices by JAX's collectives and lax.ppermute only.
A program may use at most 128 MiB of HBM per device.

v0:
```python
import math

import jax
import jax.numpy as jnp
from jax import lax
from jax.sharding import PartitionSpec as P

H = 16


def from_partner(shard, axis, stride):
    return lax.ppermute(shard, axis, [(i, i ^ 1 << stride) for i in range(lax.axis_size(axis))])


def per_device(tokens, shift_cond, scale_cond, gate_cond, qkv_weight, out_weight, cotangent):
    seq_count = lax.axis_size("seq")
    repeat = seq_count // H
    levels = repeat.bit_length() - 1
    tok_rows = tokens.shape[0]
    model_width = tokens.shape[1]
    head_size = model_width // H
    sub_rows = tok_rows // repeat
    att_scale = 1.0 / math.sqrt(head_size)
    tokens_wide = tokens.astype(jnp.float32)
    row_mean = jnp.mean(tokens_wide, axis=1, keepdims=True)
    centered = tokens_wide - row_mean
    variance = jnp.mean(centered * centered, axis=1, keepdims=True)
    inv_std = lax.rsqrt(variance + 1e-06)
    normed = centered * inv_std
    modulated = (normed * (1.0 + scale_cond) + shift_cond).astype(jnp.bfloat16)
    qkv_cols = lax.dot_general(
        qkv_weight, modulated, (((0,), (1,)), ((), ())), preferred_element_type=jnp.float32
    ).astype(jnp.bfloat16)
    qkv_grid = qkv_cols.reshape(3, H, head_size, repeat, sub_rows).transpose(0, 1, 3, 2, 4)
    qkv_grid = qkv_grid.reshape(3, seq_count, head_size, sub_rows)
    landed = lax.all_to_all(qkv_grid, "seq", split_axis=1, concat_axis=3, tiled=True)
    queries = landed[0, 0]
    key_value = landed[1:, 0]
    for level in range(levels):
        partner = from_partner(key_value, "seq", level)
        key_value = jnp.concatenate([key_value, partner], axis=2)
    key_cols = key_value[0]
    value_cols = key_value[1]
    query_len = queries.shape[1]
    key_len = key_cols.shape[1]
    block_len = math.gcd(512, query_len)
    block_count = query_len // block_len
    query_blocks = queries.reshape(head_size, block_count, block_len).transpose(1, 0, 2)

    def forward_block(query_block):
        scores = (
            lax.dot_general(
                query_block, key_cols, (((0,), (0,)), ((), ())), preferred_element_type=jnp.float32
            )
            * att_scale
        )
        row_max = jnp.max(scores, axis=1, keepdims=True)
        exponent = jnp.exp(scores - row_max)
        weights = (exponent / jnp.sum(exponent, axis=1, keepdims=True)).astype(jnp.bfloat16)
        head_result = lax.dot_general(
            value_cols, weights, (((1,), (1,)), ((), ())), preferred_element_type=jnp.float32
        ).astype(jnp.bfloat16)
        return (weights, head_result)

    weights_all, head_out = lax.map(forward_block, query_blocks)
    attended = head_out.transpose(1, 0, 2).reshape(1, head_size, query_len)
    returned = lax.all_to_all(attended, "seq", split_axis=2, concat_axis=0, tiled=True)
    attended_cols = returned.reshape(H, repeat, head_size, sub_rows).transpose(0, 2, 1, 3)
    attended_cols = attended_cols.reshape(model_width, tok_rows)
    branch = lax.dot_general(
        attended_cols, out_weight, (((0,), (0,)), ((), ())), preferred_element_type=jnp.float32
    )
    block_output = (tokens_wide + gate_cond * branch).astype(jnp.bfloat16)
    cot_wide = cotangent.astype(jnp.float32)
    gated_grad = (gate_cond * cot_wide).astype(jnp.bfloat16)
    gate_grad = jnp.sum(cot_wide * branch, axis=0)
    attended_grad = lax.dot_general(
        out_weight, gated_grad, (((1,), (1,)), ((), ())), preferred_element_type=jnp.float32
    ).astype(jnp.bfloat16)
    grad_grid = attended_grad.reshape(H, head_size, repeat, sub_rows).transpose(0, 2, 1, 3)
    grad_grid = grad_grid.reshape(seq_count, head_size, sub_rows)
    out_grads = lax.all_to_all(grad_grid, "seq", split_axis=0, concat_axis=2, tiled=True)[0]
    grad_blocks = out_grads.reshape(head_size, block_count, block_len).transpose(1, 0, 2)

    def backward_step(total_grad, block_items):
        query_block, out_block, grad_block, weight_block = block_items
        prob_grad = lax.dot_general(
            grad_block, value_cols, (((0,), (0,)), ((), ())), preferred_element_type=jnp.float32
        )
        row_delta = jnp.sum(out_block.astype(jnp.float32) * grad_block.astype(jnp.float32), axis=0)
        score_grad = (
            weight_block.astype(jnp.float32) * (prob_grad - row_delta[:, None]) * att_scale
        ).astype(jnp.bfloat16)
        query_grad = lax.dot_general(
            key_cols, score_grad, (((1,), (1,)), ((), ())), preferred_element_type=jnp.float32
        ).astype(jnp.bfloat16)
        key_grad = lax.dot_general(
            query_block, score_grad, (((1,), (0,)), ((), ())), preferred_element_type=jnp.float32
        )
        value_grad = lax.dot_general(
            grad_block, weight_block, (((1,), (0,)), ((), ())), preferred_element_type=jnp.float32
        )
        return (total_grad + jnp.stack([key_grad, value_grad]), query_grad)

    start_grad = jnp.zeros((2, head_size, key_len), jnp.float32)
    pair_grads, query_grads = lax.scan(
        backward_step, start_grad, (query_blocks, head_out, grad_blocks, weights_all)
    )
    query_grad_all = query_grads.transpose(1, 0, 2).reshape(head_size, query_len)
    for level in reversed(range(levels)):
        middle = pair_grads.shape[2] // 2
        partner = from_partner(pair_grads[:, :, middle:], "seq", level)
        pair_grads = pair_grads[:, :, :middle] + partner
    stacked = jnp.concatenate([query_grad_all[None], pair_grads.astype(jnp.bfloat16)], axis=0)
    came_back = lax.all_to_all(
        stacked.reshape(3, 1, head_size, query_len), "seq", split_axis=3, concat_axis=1, tiled=True
    )
    qkv_grad = came_back.reshape(3, H, repeat, head_size, sub_rows).transpose(0, 1, 3, 2, 4)
    qkv_grad = qkv_grad.reshape(3 * model_width, tok_rows)
    modulated_grad = lax.dot_general(
        qkv_grad, qkv_weight, (((0,), (1,)), ((), ())), preferred_element_type=jnp.float32
    )
    local_sums = jnp.stack(
        [jnp.sum(modulated_grad, axis=0), jnp.sum(modulated_grad * normed, axis=0), gate_grad]
    )
    mod_sums = lax.psum(local_sums, "seq")
    grad_condition = mod_sums / math.sqrt(tok_rows * seq_count)
    normed_grad = modulated_grad * (1.0 + scale_cond)
    first_mean = jnp.mean(normed_grad, axis=1, keepdims=True)
    second_mean = jnp.mean(normed_grad * normed, axis=1, keepdims=True)
    grad_input = (cot_wide + inv_std * (normed_grad - first_mean - normed * second_mean)).astype(
        jnp.bfloat16
    )
    return (block_output, grad_input, grad_condition)


def solution(mesh):
    return jax.shard_map(
        per_device,
        mesh=mesh,
        in_specs=(
            P(("groups", "seq"), None),
            P("groups"),
            P("groups"),
            P("groups"),
            P(),
            P(),
            P(("groups", "seq"), None),
        ),
        out_specs=(P(("groups", "seq"), None), P(("groups", "seq"), None), P("groups", None)),
        check_vma=False,
    )
```

profile of v0, /device:TPU:0, one launch (start us, length us, event | category | flops | bytes accessed | tf_op | source)
XLA Modules:
  0.0 287.5 jit_solution(3109054477897225463)
XLA Ops:
  5.2 7.4 %all-to-all-start.2 = ((bf16[16,72,128]{2,1,0:T(8,128)(2,1)}), bf16[16,72,128]{2,1,0:T(8,128)(2,1)}, u32[]{:S(2)}, u32[]{:S(2)}) async-start(bf16[16,72,128]{2,1,0:T(8,128)(2,1)} %bitcast.14), calls=%async_computation.2 | async-start | bytes 589824 | tf_op jit(solution)/shard_map/all_to_all | solution.py:82
  13.0 5.6 %fusion.21 = bf16[3456,128]{0,1:T(8,128)(2,1)} fusion(bf16[1152,3456]{1,0:T(8,128)(2,1)} %param.15, bf16[128,1152]{1,0:T(8,128)(2,1)S(1)} %copy-done.2, f32[1152]{0:T(1024)S(1)} %copy-done.6, f32[1152]{0:T(1024)S(1)} %broadcast_add_fusion, f32[128]{0:T(128)S(1)} %add_rsqrt_fusion, f32[128]{0:T(128)S(1)} %broadcast_multiply_fusion.3), kind=kOutput, calls=%fused_computation.33 | convolution fusion | flops 1020542976 | bytes 9152512 | tf_op jit(solution)/shard_map/dot_general | solution.py:31
  23.2 4.3 %all-to-all-start = ((bf16[3,16,72,128]{3,2,0,1:T(8,128)(2,1)}), bf16[3,16,72,128]{3,2,0,1:T(8,128)(2,1)S(1)}, u32[]{:S(2)}, u32[]{:S(2)}) async-start(bf16[3,16,72,128]{3,2,0,1:T(8,128)(2,1)} %copy.72), calls=%async_computation | async-start | bytes 1769472 | tf_op jit(solution)/shard_map/all_to_all | solution.py:36
  32.8 15.0 %all-to-all-done = bf16[3,16,72,128]{3,2,0,1:T(8,128)(2,1)S(1)} async-done(((bf16[3,16,72,128]{3,2,0,1:T(8,128)(2,1)}), bf16[3,16,72,128]{3,2,0,1:T(8,128)(2,1)S(1)}, u32[]{:S(2)}, u32[]{:S(2)}) %all-to-all-start) | async-done | bytes 884768 | tf_op jit(solution)/shard_map/all_to_all | solution.py:36
  53.0 28.4 %while.25 = (s32[]{:T(128)}, bf16[4,512,2048]{2,1,0:T(8,128)(2,1)}, bf16[4,72,512]{2,1,0:T(8,128)(2,1)}, bf16[4,72,512]{2,1,0:T(8,128)(2,1)}, bf16[72,2048]{1,0:...) while((s32[]{:T(128)}, bf16[4,512,2048]{2,1,0:T(8,128)(2,1)}, bf16[4,72,512]{2,1,0:T(8,128)(2,1)}, ...), condition=%wide.region_5.6_spmd, body=%wide.region_2.5_spmd.sunk | while | flops 311462912 | bytes 19623500 | solution.py:65
  82.1 59.1 %while.26 = (s32[]{:T(128)}, f32[2,72,2048]{2,1,0:T(8,128)}, bf16[4,72,512]{2,1,0:T(8,128)(2,1)}, bf16[4,72,512]{2,1,0:T(8,128)(2,1)}, bf16[4,512,2048]{2,1,0:T(...) while((s32[]{:T(128)}, f32[2,72,2048]{2,1,0:T(8,128)}, ...), condition=%wide.region_8.9_spmd.clone, body=%wide.region_6.8_spmd.clone.sunk | while | flops 610291200 | bytes 24632472 | solution.py:106
  93.6 3.0 %fusion.90 = bf16[4,72,512]{2,1,0:T(8,128)(2,1)} fusion(bf16[4,72,512]{2,1,0:T(8,128)(2,1)} %get-tuple-element.374, s32[]{:T(128)} %get-tuple-element.372, bf16[512,2048]{1,0:T(8,128)(2,1)} %copy-done.1, bf16[72,2048]{1,0:T(8,128)(2,1)S(1)} %get-tuple-element.391), kind=kOutput, calls=%fused_computation.20.clone.1 | convolution fusion | flops 151031808 | bytes 2466304 | tf_op jit(solution)/shard_map/while/body/eval_jaxpr/dot_general | solution.py:94
  105.8 2.6 maximum_add_fusion.2
  108.4 3.0 %fusion.90 = bf16[4,72,512]{2,1,0:T(8,128)(2,1)} fusion(bf16[4,72,512]{2,1,0:T(8,128)(2,1)} %get-tuple-element.374, s32[]{:T(128)} %get-tuple-element.372, bf16[512,2048]{1,0:T(8,128)(2,1)} %copy-done.1, bf16[72,2048]{1,0:T(8,128)(2,1)S(1)} %get-tuple-element.391), kind=kOutput, calls=%fused_computation.20.clone.1 | convolution fusion | flops 151031808 | bytes 2466304 | tf_op jit(solution)/shard_map/while/body/eval_jaxpr/dot_general | solution.py:94
  120.7 2.6 maximum_add_fusion.2
  123.3 3.0 %fusion.90 = bf16[4,72,512]{2,1,0:T(8,128)(2,1)} fusion(bf16[4,72,512]{2,1,0:T(8,128)(2,1)} %get-tuple-element.374, s32[]{:T(128)} %get-tuple-element.372, bf16[512,2048]{1,0:T(8,128)(2,1)} %copy-done.1, bf16[72,2048]{1,0:T(8,128)(2,1)S(1)} %get-tuple-element.391), kind=kOutput, calls=%fused_computation.20.clone.1 | convolution fusion | flops 151031808 | bytes 2466304 | tf_op jit(solution)/shard_map/while/body/eval_jaxpr/dot_general | solution.py:94
  135.6 2.6 maximum_add_fusion.2
  138.2 3.0 %fusion.90 = bf16[4,72,512]{2,1,0:T(8,128)(2,1)} fusion(bf16[4,72,512]{2,1,0:T(8,128)(2,1)} %get-tuple-element.374, s32[]{:T(128)} %get-tuple-element.372, bf16[512,2048]{1,0:T(8,128)(2,1)} %copy-done.1, bf16[72,2048]{1,0:T(8,128)(2,1)S(1)} %get-tuple-element.391), kind=kOutput, calls=%fused_computation.20.clone.1 | convolution fusion | flops 151031808 | bytes 2466304 | tf_op jit(solution)/shard_map/while/body/eval_jaxpr/dot_general | solution.py:94
  148.8 12.8 %reduce = bf16[2048,72]{1,0:T(8,128)(2,1)S(1)} reduce(bf16[2048,1,72]{2,1,0:T(2,128)(2,1)} %bitcast.144, bf16[]{:T(256)} %broadcast.71), dimensions={1}, to_apply=%bitcast.81.reduce_sub_computation | reduce | bytes 589826
  163.4 6.0 %all-to-all-start.1 = ((bf16[16,2,4608]{2,1,0:T(2,128)(2,1)}), bf16[16,2,4608]{2,1,0:T(2,128)(2,1)}, u32[]{:S(2)}, u32[]{:S(2)}) async-start(bf16[16,2,4608]{2,1,0:T(2,128)(2,1)} %reshape.56), calls=%async_computation.1 | async-start | bytes 589824 | tf_op jit(solution)/shard_map/all_to_all | solution.py:67
  173.2 3.0 %bitcast_bitcast_fusion.1 = bf16[2048,1,3,72]{3,2,1,0:T(4,128)(2,1)} fusion(bf16[3,72,2048]{1,0,2:T(4,128)(2,1)} %copy.86), kind=kLoop, calls=%fused_computation.77 | loop fusion | bytes 1769472
  176.2 5.0 %reshape.58 = bf16[16,2,13824]{2,1,0:T(2,128)(2,1)} reshape(bf16[2048,1,3,72]{3,2,1,0:T(4,128)(2,1)} %bitcast_bitcast_fusion.1) | data formatting | bytes 1769472
  181.2 6.0 %all-to-all-start.3 = ((bf16[16,2,13824]{2,1,0:T(2,128)(2,1)}), bf16[16,2,13824]{2,1,0:T(2,128)(2,1)}, u32[]{:S(2)}, u32[]{:S(2)}) async-start(bf16[16,2,13824]{2,1,0:T(2,128)(2,1)} %reshape.58), calls=%async_computation.3 | async-start | bytes 1769472 | tf_op jit(solution)/shard_map/all_to_all | solution.py:115
  187.2 4.1 %reshape.57 = bf16[2048,1,72]{2,1,0:T(2,128)(2,1)} reshape(bf16[16,2,4608]{2,1,0:T(2,128)(2,1)} %all-to-all-done.1) | data formatting | bytes 589824
  193.8 13.8 %all-to-all-done.3 = bf16[16,2,13824]{2,1,0:T(2,128)(2,1)} async-done(((bf16[16,2,13824]{2,1,0:T(2,128)(2,1)}), bf16[16,2,13824]{2,1,0:T(2,128)(2,1)}, u32[]{:S(2)}, u32[]{:S(2)}) %all-to-all-start.3) | async-done | bytes 884768 | tf_op jit(solution)/shard_map/all_to_all | solution.py:115
  207.6 5.4 %reshape.59 = bf16[2048,1,3,72]{3,2,1,0:T(4,128)(2,1)} reshape(bf16[16,2,13824]{2,1,0:T(2,128)(2,1)} %all-to-all-done.3) | data formatting | bytes 1769472
  213.0 3.9 %copy.91 = bf16[3,1,72,16,128]{4,2,3,0,1:T(8,128)(2,1)} copy(bf16[3,1,72,16,128]{2,0,4,3,1:T(4,128)(2,1)} %bitcast.143) | data formatting | bytes 1769472 | tf_op jit(solution)/shard_map/all_to_all | solution.py:115
  216.9 6.2 %fusion.34 = (f32[1152]{0:T(1024)S(1)}, f32[128]{0:T(128)S(1)}, f32[128]{0:T(128)S(1)}, f32[1152]{0:T(1024)S(1)}, f32[128,1152]{1,0:T(8,128)S(1)}) fusion(bf16[128,1152]{1,0:T(8,128)(2,1)S(1)} %copy-done.3, f32[128]{0:T(128)S(1)} %add_rsqrt_fusion, f32[128]{0:T(128)S(1)} %broadcast_multiply_fusion.3, f32[1152]{0:T(1024)S(1)} %broadcast_add_fusion, ...), kind=kOutput, calls=%fused_computation.54 | convolution fusion | flops 1020687872 | bytes 9747968 | tf_op jit(solution)/shard_map/dot_general | solution.py:120
  224.9 62.0 %psum.7 = f32[3,1152]{1,0:T(4,128)S(1)} all-reduce(f32[3,1152]{1,0:T(4,128)S(1)} %pad_maximum_fusion.1), channel_id=1, replica_groups=mesh['groups'=2,'seq'=16] {'seq'}, use_global_device_ids=true, to_apply=%region_14.15 | all-reduce | flops 3456 | bytes 27648 | tf_op jit(solution)/shard_map/psum | solution.py:126
  (101 shorter events, 106.0 us)
Async XLA Ops:
  0.6 1.8 copy-start
  0.6 12.0 %copy-start.2 = (bf16[128,1152]{1,0:T(8,128)(2,1)S(1)}, bf16[128,1152]{1,0:T(8,128)(2,1)}, u32[]{:S(2)}) copy-start(bf16[128,1152]{1,0:T(8,128)(2,1)} %param.11) | copy-start | bytes 884740
  0.7 12.3 %copy-start.7 = (f32[1152]{0:T(1024)S(1)}, f32[1152]{0:T(1024)}, u32[]{:S(2)}) copy-start(f32[1152]{0:T(1024)} %param.13) | copy-start | bytes 13828
  0.7 12.3 %copy-start.6 = (f32[1152]{0:T(1024)S(1)}, f32[1152]{0:T(1024)}, u32[]{:S(2)}) copy-start(f32[1152]{0:T(1024)} %param.12) | copy-start | bytes 13828
  5.2 18.1 %all-to-all-start.2 = ((bf16[16,72,128]{2,1,0:T(8,128)(2,1)}), bf16[16,72,128]{2,1,0:T(8,128)(2,1)}, u32[]{:S(2)}, u32[]{:S(2)}) async-start(bf16[16,72,128]{2,1,0:T(8,128)(2,1)} %bitcast.14), calls=%async_computation.2 | async-start | bytes 589824 | tf_op jit(solution)/shard_map/all_to_all | solution.py:82
  23.2 24.6 %all-to-all-start = ((bf16[3,16,72,128]{3,2,0,1:T(8,128)(2,1)}), bf16[3,16,72,128]{3,2,0,1:T(8,128)(2,1)S(1)}, u32[]{:S(2)}, u32[]{:S(2)}) async-start(bf16[3,16,72,128]{3,2,0,1:T(8,128)(2,1)} %copy.72), calls=%async_computation | async-start | bytes 1769472 | tf_op jit(solution)/shard_map/all_to_all | solution.py:36
  85.6 1.4 copy-start.1
  100.1 1.4 copy-start.1
  115.0 1.4 copy-start.1
  129.8 1.4 copy-start.1
  163.4 17.8 %all-to-all-start.1 = ((bf16[16,2,4608]{2,1,0:T(2,128)(2,1)}), bf16[16,2,4608]{2,1,0:T(2,128)(2,1)}, u32[]{:S(2)}, u32[]{:S(2)}) async-start(bf16[16,2,4608]{2,1,0:T(2,128)(2,1)} %reshape.56), calls=%async_computation.1 | async-start | bytes 589824 | tf_op jit(solution)/shard_map/all_to_all | solution.py:67
  181.2 26.4 %all-to-all-start.3 = ((bf16[16,2,13824]{2,1,0:T(2,128)(2,1)}), bf16[16,2,13824]{2,1,0:T(2,128)(2,1)}, u32[]{:S(2)}, u32[]{:S(2)}) async-start(bf16[16,2,13824]{2,1,0:T(2,128)(2,1)} %reshape.58), calls=%async_computation.3 | async-start | bytes 1769472 | tf_op jit(solution)/shard_map/all_to_all | solution.py:115
  193.6 23.3 %copy-start.3 = (bf16[128,1152]{1,0:T(8,128)(2,1)S(1)}, bf16[128,1152]{1,0:T(8,128)(2,1)}, u32[]{:S(2)}) copy-start(bf16[128,1152]{1,0:T(8,128)(2,1)} %param.11) | copy-start | bytes 884740
  216.9 6.3 %copy-start.4 = (bf16[128,1152]{1,0:T(8,128)(2,1)S(1)}, bf16[128,1152]{1,0:T(8,128)(2,1)}, u32[]{:S(2)}) copy-start(bf16[128,1152]{1,0:T(8,128)(2,1)} %param.17) | copy-start | bytes 884740
  216.9 6.3 %copy-start.5 = (f32[1152]{0:T(1024)S(1)}, f32[1152]{0:T(1024)}, u32[]{:S(2)}) copy-start(f32[1152]{0:T(1024)} %param.14) | copy-start | bytes 13828
where the time goes:
time: 290 us; the launch traced here: 288 us
  matrix products  71.2 us (25%)
  blocking collectives  62 us (21%)
  local copies, waits for them, and re-layouts  55.9 us (19%)
  other arithmetic  43.2 us (15%)
  waiting for transfers between devices  30.4 us (10%)
  starting transfers between devices  23.8 us (8%)
    psum x1, blocking collectives, per_device(): mod_sums = lax.psum(local_sums, 'seq')  62 us
    unnamed x22, local copies, waits for them, and re-layouts  23.4 us
    all_to_all x1, waiting for transfers between devices, per_device(): lax.all_to_all(qkv_grid, 'seq', split_axis=1, concat_axis=3, tiled=True)  15 us
    all_to_all x1, waiting for transfers between devices, per_device(): lax.all_to_all(stacked.reshape(3, 1, head_size, query_len), 'seq', split_...  13.8 us
    unnamed x2, other arithmetic  12.8 us
    dot_general x4, matrix products, backward_step(): lax.dot_general(key_cols, score_grad, (((1,), (1,)), ((), ())), preferred...  12 us
    dot_general x4, matrix products, backward_step(): lax.dot_general(grad_block, value_cols, (((0,), (0,)), ((), ())), preferr...  10.3 us
    add x4, other arithmetic, backward_step(): return (total_grad + jnp.stack([key_grad, value_grad]), query_grad)  10.1 us
  transfers between devices with their start and end apart: 4, of which 3 were waited for; matrix products, arithmetic and copies ran while one was open for 11% of the time, Pallas kernels for 0%

commit v1 on v0

v1 whole, which is shorter than its diff:
```python
import functools
import math

import jax
import jax.numpy as jnp
from jax import lax
from jax.experimental import pallas as pl
from jax.experimental.pallas import tpu as pltpu
from jax.sharding import PartitionSpec as P

H = 16
LANES = 128
F32 = jnp.float32
BF16 = jnp.bfloat16
VMEM_LIMIT = 56 * 1024 * 1024


def params():
    return pltpu.CompilerParams(
        dimension_semantics=("arbitrary",), vmem_limit_bytes=VMEM_LIMIT
    )


def normalise(tokens):
    wide = tokens.astype(F32)
    row_mean = jnp.mean(wide, axis=1, keepdims=True)
    centered = wide - row_mean
    variance = jnp.mean(centered * centered, axis=1, keepdims=True)
    inv_std = lax.rsqrt(variance + 1e-06)
    return wide, centered * inv_std, inv_std


def project_kernel(
    head_size, tokens, shift, scale, gate, qkv_w, out_w, cot, packed, modulated, gated, flat
):
    step = pl.program_id(0)
    width = tokens.shape[1]
    tile = qkv_w.shape[1]
    rows = out_w.shape[0]

    @pl.when(step == 0)
    def _():
        _, normed, _ = normalise(tokens[...])
        modulated[...] = (normed * (1.0 + scale[...]) + shift[...]).astype(BF16)
        gated[...] = (gate[...] * cot[...].astype(F32)).astype(BF16)

    cols = jnp.dot(modulated[...], qkv_w[...], preferred_element_type=F32)
    flat[pl.ds(pl.multiple_of(step * tile, LANES), tile), :] = cols.T
    flat[pl.ds(pl.multiple_of(3 * width + step * rows, LANES), rows), :] = lax.dot_general(
        out_w[...], gated[...], (((1,), (1,)), ((), ())), preferred_element_type=F32
    )

    @pl.when(step == pl.num_programs(0) - 1)
    def _():
        for head in range(H):
            packed[head] = jnp.concatenate(
                [
                    flat[part * width + head * head_size : part * width + (head + 1) * head_size, :]
                    for part in range(4)
                ],
                axis=0,
            ).astype(BF16)


def project(tokens, shift, scale, gate, qkv_w, out_w, cot):
    tok_rows, width = tokens.shape
    steps = width // LANES
    head_size = width // H
    tile = 3 * LANES
    whole = lambda shape: pl.BlockSpec(shape, lambda i: (0,) * len(shape))
    return pl.pallas_call(
        functools.partial(project_kernel, head_size),
        grid=(steps,),
        in_specs=[
            whole((tok_rows, width)),
            whole((1, width)),
            whole((1, width)),
            whole((1, width)),
            pl.BlockSpec((width, tile), lambda i: (0, i)),
            pl.BlockSpec((LANES, width), lambda i: (i, 0)),
            whole((tok_rows, width)),
        ],
        out_specs=whole((H, 4 * head_size, tok_rows)),
        out_shape=jax.ShapeDtypeStruct((H, 4 * head_size, tok_rows), BF16),
        scratch_shapes=[
            pltpu.VMEM((tok_rows, width), BF16),
            pltpu.VMEM((tok_rows, width), BF16),
            pltpu.VMEM((4 * width, tok_rows), F32),
        ],
        compiler_params=params(),
        name="project",
    )(tokens, shift, scale, gate, qkv_w, out_w, cot)


def attend_kernel(head_size, group, split, items, *refs):
    if split:
        pairs, near, far = refs[:3]
        refs = refs[3:]
    else:
        near = refs[0]
        refs = refs[1:]
    key_rows, value_rows, key_cols, value_cols, key_grad, value_grad, near_flat = refs
    step = pl.program_id(0)
    chunks = items.shape[0]
    key_chunks = key_rows.shape[0] // LANES
    att_scale = 1.0 / math.sqrt(head_size)
    pad = value_rows.shape[1] - head_size

    @pl.when(step == 0)
    def _():
        for s in range(key_chunks):
            if split:
                pair = pairs[s].astype(F32)
            else:
                pair = items[s].astype(F32)[head_size : 3 * head_size]
            at = slice(s * LANES, (s + 1) * LANES)
            keys, values = pair[:head_size], pair[head_size:]
            key_cols[:, at] = keys.astype(BF16)
            value_cols[:, at] = values.astype(BF16)
            key_rows[at, :] = keys.T.astype(BF16)
            value_rows[at, :] = jnp.concatenate(
                [values, jnp.ones((pad, LANES), F32)], axis=0
            ).T.astype(BF16)
        key_grad[...] = jnp.zeros_like(key_grad)
        value_grad[...] = jnp.zeros_like(value_grad)

    block = [items[step * group + g].astype(F32) for g in range(group)]
    queries = jnp.concatenate([b[:head_size] for b in block], axis=1)
    grads = jnp.concatenate([b[3 * head_size :] for b in block], axis=1)
    scores = jnp.dot(key_rows[...], queries.astype(BF16), preferred_element_type=F32) * att_scale
    row_max = jnp.max(scores, axis=0, keepdims=True)
    exponent = jnp.exp(scores - row_max)
    total = jnp.sum(exponent, axis=0, keepdims=True)
    weights = (exponent * (1.0 / total)).astype(BF16)
    attended = (
        jnp.dot(value_cols[...], weights, preferred_element_type=F32).astype(BF16).astype(F32)
    )
    less = -jnp.sum(attended * grads, axis=0, keepdims=True)
    less_high = less.astype(BF16).astype(F32)
    less_mid = (less - less_high).astype(BF16).astype(F32)
    less_low = less - less_high - less_mid
    place = lax.broadcasted_iota(jnp.int32, (pad, less.shape[1]), 0)
    tail = jnp.where(
        place == 0, less_high, jnp.where(place == 1, less_mid, jnp.where(place == 2, less_low, 0.0))
    )
    centred_grad = jnp.dot(
        value_rows[...],
        jnp.concatenate([grads, tail], axis=0).astype(BF16),
        preferred_element_type=F32,
    )
    score_grad = (weights.astype(F32) * centred_grad * att_scale).astype(BF16)
    query_grad = jnp.dot(key_cols[...], score_grad, preferred_element_type=F32)
    key_grad[...] += jnp.dot(score_grad, queries.T.astype(BF16), preferred_element_type=F32)
    value_grad[...] += jnp.dot(weights, grads.T.astype(BF16), preferred_element_type=F32)
    for g in range(group):
        at = slice(g * LANES, (g + 1) * LANES)
        near_flat[step * group + g] = jnp.concatenate(
            [attended[:, at], query_grad[:, at]], axis=0
        )

    @pl.when(step == pl.num_programs(0) - 1)
    def _():
        for s in range(key_chunks):
            at = slice(s * LANES, (s + 1) * LANES)
            grads_of = jnp.concatenate([key_grad[at, :].T, value_grad[at, :].T], axis=0)
            if split:
                far[s] = grads_of
            else:
                near[s] = jnp.concatenate([near_flat[s], grads_of], axis=0).astype(BF16)
        if split:
            near[...] = near_flat[...].astype(BF16)


def attend(items, pairs=None):
    chunks = items.shape[0]
    head_size = items.shape[1] // 4
    split = pairs is not None
    key_chunks = pairs.shape[0] if split else chunks
    group = 2 if chunks % 2 == 0 else 1
    key_len = key_chunks * LANES
    pad = 8
    whole = lambda shape: pl.BlockSpec(shape, lambda i: (0,) * len(shape))
    if split:
        shapes = [
            jax.ShapeDtypeStruct((chunks, 2 * head_size, LANES), BF16),
            jax.ShapeDtypeStruct((key_chunks, 2 * head_size, LANES), F32),
        ]
        operands = (items, pairs)
    else:
        shapes = [jax.ShapeDtypeStruct((chunks, 4 * head_size, LANES), BF16)]
        operands = (items,)
    return pl.pallas_call(
        functools.partial(attend_kernel, head_size, group, split),
        grid=(chunks // group,),
        in_specs=[whole(x.shape) for x in operands],
        out_specs=[whole(x.shape) for x in shapes],
        out_shape=shapes,
        scratch_shapes=[
            pltpu.VMEM((key_len, head_size), BF16),
            pltpu.VMEM((key_len, head_size + pad), BF16),
            pltpu.VMEM((head_size, key_len), BF16),
            pltpu.VMEM((head_size, key_len), BF16),
            pltpu.VMEM((key_len, head_size), F32),
            pltpu.VMEM((key_len, head_size), F32),
            pltpu.VMEM((chunks, 2 * head_size, LANES), F32),
        ],
        compiler_params=params(),
        name="attend",
    )(*operands)


def finish_kernel(
    head_size, items, tokens, scale, gate, qkv_w, out_w, cot,
    block_output, grad_input, sums, att_cols, grad_cols, branch, mod_grad,
):
    step = pl.program_id(0)
    width = tokens.shape[1]
    rows = qkv_w.shape[0]

    @pl.when(step == 0)
    def _():
        flat = [items[head].astype(F32) for head in range(H)]
        att = jnp.concatenate([x[:head_size] for x in flat], axis=0)
        for part in range(width // LANES):
            att_cols[part] = att[part * LANES : (part + 1) * LANES, :].T.astype(BF16)
        for part in range(3):
            grad_cols[part * width : (part + 1) * width, :] = jnp.concatenate(
                [x[(part + 1) * head_size : (part + 2) * head_size] for x in flat], axis=0
            ).astype(BF16)
        branch[...] = jnp.zeros_like(branch)

    branch[...] += jnp.dot(att_cols[step], out_w[...], preferred_element_type=F32)
    mod_grad[step] = jnp.dot(qkv_w[...], grad_cols[...], preferred_element_type=F32).T

    @pl.when(step == pl.num_programs(0) - 1)
    def _():
        wide, normed, inv_std = normalise(tokens[...])
        cot_wide = cot[...].astype(F32)
        out = branch[...]
        block_output[...] = (wide + gate[...] * out).astype(BF16)
        back = jnp.concatenate([mod_grad[i] for i in range(width // rows)], axis=1)
        sums[...] = jnp.concatenate(
            [
                jnp.sum(back, axis=0, keepdims=True),
                jnp.sum(back * normed, axis=0, keepdims=True),
                jnp.sum(cot_wide * out, axis=0, keepdims=True),
            ],
            axis=0,
        )
        normed_grad = back * (1.0 + scale[...])
        first_mean = jnp.mean(normed_grad, axis=1, keepdims=True)
        second_mean = jnp.mean(normed_grad * normed, axis=1, keepdims=True)
        grad_input[...] = (
            cot_wide + inv_std * (normed_grad - first_mean - normed * second_mean)
        ).astype(BF16)


def finish(items, tokens, scale, gate, qkv_w, out_w, cot):
    tok_rows, width = tokens.shape
    head_size = width // H
    steps = width // LANES
    whole = lambda shape: pl.BlockSpec(shape, lambda i: (0,) * len(shape))
    return pl.pallas_call(
        functools.partial(finish_kernel, head_size),
        grid=(steps,),
        in_specs=[
            whole(items.shape),
            whole((tok_rows, width)),
            whole((1, width)),
            whole((1, width)),
            pl.BlockSpec((LANES, 3 * width), lambda i: (i, 0)),
            pl.BlockSpec((LANES, width), lambda i: (i, 0)),
            whole((tok_rows, width)),
        ],
        out_specs=[whole((tok_rows, width)), whole((tok_rows, width)), whole((3, width))],
        out_shape=[
            jax.ShapeDtypeStruct((tok_rows, width), BF16),
            jax.ShapeDtypeStruct((tok_rows, width), BF16),
            jax.ShapeDtypeStruct((3, width), F32),
        ],
        scratch_shapes=[
            pltpu.VMEM((steps, tok_rows, LANES), BF16),
            pltpu.VMEM((3 * width, tok_rows), BF16),
            pltpu.VMEM((tok_rows, width), F32),
            pltpu.VMEM((steps, tok_rows, LANES), F32),
        ],
        compiler_params=params(),
        name="finish",
    )(items, tokens, scale, gate, qkv_w, out_w, cot)


def from_partner(shard, axis, stride):
    return lax.ppermute(shard, axis, [(i, i ^ stride) for i in range(lax.axis_size(axis))])


def exchange(blocks):
    return lax.all_to_all(blocks, "seq", split_axis=0, concat_axis=0, tiled=True)


def per_device(tokens, shift_cond, scale_cond, gate_cond, qkv_weight, out_weight, cotangent):
    seq_count = lax.axis_size("seq")
    repeat = seq_count // H
    levels = repeat.bit_length() - 1
    tok_rows, width = tokens.shape
    head_size = width // H
    sub_rows = tok_rows // repeat
    shift, scale, gate = (x.reshape(1, width) for x in (shift_cond, scale_cond, gate_cond))
    packed = project(tokens, shift, scale, gate, qkv_weight, out_weight, cotangent)
    if repeat == 1:
        (made,) = attend(exchange(packed))
        returned = exchange(made)
    else:
        packed = packed.reshape(H, 4 * head_size, repeat, sub_rows).transpose(0, 2, 1, 3)
        landed = exchange(packed.reshape(seq_count, 4 * head_size, sub_rows))
        items = landed.reshape(H, repeat, 4 * head_size, sub_rows).transpose(0, 2, 1, 3)
        items = items.reshape(H, 4 * head_size, tok_rows)
        pairs = items[:, head_size : 3 * head_size]
        for level in range(levels):
            pairs = jnp.concatenate([pairs, from_partner(pairs, "seq", 1 << level)], axis=0)
        near, far = attend(items, pairs)
        for level in reversed(range(levels)):
            middle = far.shape[0] // 2
            far = far[:middle] + from_partner(far[middle:], "seq", 1 << level)
        made = jnp.concatenate([near, far.astype(BF16)], axis=1)
        made = made.reshape(H, 4 * head_size, repeat, sub_rows).transpose(0, 2, 1, 3)
        back = exchange(made.reshape(seq_count, 4 * head_size, sub_rows))
        returned = back.reshape(H, repeat, 4 * head_size, sub_rows).transpose(0, 2, 1, 3)
        returned = returned.reshape(H, 4 * head_size, tok_rows)
    block_output, grad_input, sums = finish(
        returned, tokens, scale, gate, qkv_weight, out_weight, cotangent
    )
    stride = 1
    while stride < seq_count:
        sums = sums + from_partner(sums, "seq", stride)
        stride *= 2
    grad_condition = sums / math.sqrt(tok_rows * seq_count)
    return (block_output, grad_input, grad_condition)


def solution(mesh):
    return jax.shard_map(
        per_device,
        mesh=mesh,
        in_specs=(
            P(("groups", "seq"), None),
            P("groups"),
            P("groups"),
            P("groups"),
            P(),
            P(),
            P(("groups", "seq"), None),
        ),
        out_specs=(P(("groups", "seq"), None), P(("groups", "seq"), None), P("groups", None)),
        check_vma=False,
    )
```

time: 290 us -> 140 us (0.48)
  matrix products: 71.2 us -> 0 us
  local copies, waits for them, and re-layouts: 55.9 us -> 3.87 us
  Pallas kernels: 0 us -> 48.9 us
  other arithmetic: 43.2 us -> 1.35 us
  starting transfers between devices: 23.8 us -> 3.24 us
  waiting for transfers between devices: 30.4 us -> 10.3 us
  blocking collectives: 62 us -> 70.8 us
    dot_general x28 -> x0, matrix products: 71.2 us -> none  [the longest x4 12 us: backward_step(): lax.dot_general(key_cols, score_grad, (((1,), (1,)), ((), ())), preferred...]
    all_to_all x0 -> x2, blocking collectives: none -> 70.8 us  [exchange(): lax.all_to_all(blocks, 'seq', split_axis=0, concat_axis=0, tiled=True)]
    psum x1 -> x0, blocking collectives: 62 us -> none  [per_device(): mod_sums = lax.psum(local_sums, 'seq')]
    pallas_call x0 -> x3, Pallas kernels: none -> 48.9 us  [the longest x1 27.3 us: attend(): pl.pallas_call(functools.partial(attend_kernel, head_size, group, split),...]
    all_to_all x4 -> x0, waiting for transfers between devices: 30.4 us -> none  [the longest x1 15 us: per_device(): lax.all_to_all(qkv_grid, 'seq', split_axis=1, concat_axis=3, tiled=True)]
    all_to_all x4 -> x0, starting transfers between devices: 23.8 us -> none  [the longest x1 7.42 us: per_device(): lax.all_to_all(grad_grid, 'seq', split_axis=0, concat_axis=2, tiled=True)[0]]
    unnamed x22 -> x0, local copies, waits for them, and re-layouts: 23.4 us -> none
    unnamed x2 -> x0, other arithmetic: 12.8 us -> none
  transfers between devices with their start and end apart: 4 -> 4, of which waited for: 3 -> 4; matrix products, arithmetic and copies ran while one was open for 11% -> 0% of each run, Pallas kernels for 0% -> 0%
where the time goes in v1:
time: 140 us; the launch traced here: 139 us
  blocking collectives  70.8 us (51%)
  Pallas kernels  48.9 us (35%)
  waiting for transfers between devices  10.3 us (7%)
  local copies, waits for them, and re-layouts  3.87 us (3%)
  starting transfers between devices  3.24 us (2%)
    all_to_all x2, blocking collectives, exchange(): lax.all_to_all(blocks, 'seq', split_axis=0, concat_axis=0, tiled=True)  70.8 us
    pallas_call x1, Pallas kernels, attend(): pl.pallas_call(functools.partial(attend_kernel, head_size, group, split),...  27.3 us
    pallas_call x1, Pallas kernels, finish(): pl.pallas_call(functools.partial(finish_kernel, head_size), grid=(steps,)...  11.3 us
    ppermute x4, waiting for transfers between devices, from_partner(): lax.ppermute(shard, axis, [(i, i ^ stride) for i in range(lax.axis_size(a...  10.3 us
    pallas_call x1, Pallas kernels, project(): pl.pallas_call(functools.partial(project_kernel, head_size), grid=(steps,...  10.3 us
    reshape x3, local copies, waits for them, and re-layouts, per_device(): x.reshape(1, width)  3.87 us
    ppermute x4, starting transfers between devices, from_partner(): lax.ppermute(shard, axis, [(i, i ^ stride) for i in range(lax.axis_size(a...  3.24 us
  transfers between devices with their start and end apart: 4, of which 4 were waited for; matrix products, arithmetic and copies ran while one was open for 0% of the time, Pallas kernels for 0%

profile of v1, /device:TPU:0, one launch (start us, length us, event | category | flops | bytes accessed | tf_op | source)
XLA Modules:
  0.0 139.2 jit_solution(11343411660293286603)
XLA Ops:
  0.6 1.3 reshape.16.scale
  1.9 1.3 reshape.17.gate
  3.2 1.3 reshape.15.shift
  4.5 10.3 %project.1 = bf16[16,288,128]{2,1,0:T(8,128)(2,1)} custom-call(bf16[128,1152]{1,0:T(8,128)(2,1)} %tokens.3, f32[1,1152]{1,0:T(1,128)} %reshape.15.shift, f32[1,1152]{1,0:T(1,128)} %reshape.16.scale, f32[1,1152]{1,0:T(1,128)} %reshape.17.gate, bf16[1152,3456]{1,0:T(8,128)(2,1)} %qkv_w.3, bf16[1152,1152]{1,0:T(8,128)(2,1)} %out_w.3, bf16[128,1152]{1,0:T(8,128)(2,1)} %cot.3), custom_call_target="tpu_custom_call" | custom-call | tf_op jit(solution)/shard_map/project/pallas_call | solution.py:71
  14.8 37.0 %all_to_all.10.items = bf16[16,288,128]{2,1,0:T(8,128)(2,1)} all-to-all(bf16[16,288,128]{2,1,0:T(8,128)(2,1)} %project.1), channel_id=1, replica_groups=mesh['groups'=2,'seq'=16] {'seq'}, dimensions={0} | all-to-all | bytes 2359296 | tf_op jit(solution)/shard_map/all_to_all | solution.py:297
  51.8 27.3 %attend.1 = bf16[16,288,128]{2,1,0:T(8,128)(2,1)} custom-call(bf16[16,288,128]{2,1,0:T(8,128)(2,1)} %all_to_all.10.items), custom_call_target="tpu_custom_call" | custom-call | tf_op jit(solution)/shard_map/attend/pallas_call | solution.py:192
  79.2 33.8 %all_to_all.11.items = bf16[16,288,128]{2,1,0:T(8,128)(2,1)} all-to-all(bf16[16,288,128]{2,1,0:T(8,128)(2,1)} %attend.1), channel_id=1, replica_groups=mesh['groups'=2,'seq'=16] {'seq'}, dimensions={0} | all-to-all | bytes 2359296 | tf_op jit(solution)/shard_map/all_to_all | solution.py:297
  113.0 11.3 %finish.1 = (bf16[128,1152]{1,0:T(8,128)(2,1)}, bf16[128,1152]{1,0:T(8,128)(2,1)}, f32[3,1152]{1,0:T(4,128)}) custom-call(bf16[16,288,128]{2,1,0:T(8,128)(2,1)} %all_to_all.11.items, bf16[128,1152]{1,0:T(8,128)(2,1)} %tokens.3, f32[1,1152]{1,0:T(1,128)} %reshape.16.scale, f32[1,1152]{1,0:T(1,128)} %reshape.17.gate, bf16[1152,3456]{1,0:T(8,128)(2,1)} %qkv_w.3, ...), custom_call_target="tpu_custom_call" | custom-call | tf_op jit(solution)/shard_map/finish/pallas_call | solution.py:263
  124.2 0.3 collective-permute-start
  124.6 1.1 collective-permute-done
  125.6 0.7 add.12
  126.4 0.7 collective-permute-start.1
  127.1 3.0 %collective-permute-done.1 = f32[3,1152]{1,0:T(4,128)S(1)} collective-permute-done((f32[3,1152]{1,0:T(4,128)S(1)}, f32[3,1152]{1,0:T(4,128)S(1)}, u32[]{:S(2)}, u32[]{:S(2)}) %collective-permute-start.1) | collective-permute-done | bytes 13856 | tf_op jit(solution)/shard_map/ppermute | solution.py:293
  130.1 0.9 collective-permute-start.2
  131.0 2.9 %collective-permute-done.2 = f32[3,1152]{1,0:T(4,128)S(1)} collective-permute-done((f32[3,1152]{1,0:T(4,128)S(1)}, f32[3,1152]{1,0:T(4,128)S(1)}, u32[]{:S(2)}, u32[]{:S(2)}) %collective-permute-start.2) | collective-permute-done | bytes 13856 | tf_op jit(solution)/shard_map/ppermute | solution.py:293
  133.9 1.3 collective-permute-start.3
  135.2 3.4 %collective-permute-done.3 = f32[3,1152]{1,0:T(4,128)S(1)} collective-permute-done((f32[3,1152]{1,0:T(4,128)S(1)}, f32[3,1152]{1,0:T(4,128)S(1)}, u32[]{:S(2)}, u32[]{:S(2)}) %collective-permute-start.3) | collective-permute-done | bytes 13856 | tf_op jit(solution)/shard_map/ppermute | solution.py:293
  138.6 0.6 add_multiply_fusion
  (2 shorter events, 0.0 us)
Async XLA Ops:
  124.2 1.4 %collective-permute-start = (f32[3,1152]{1,0:T(4,128)}, f32[3,1152]{1,0:T(4,128)S(1)}, u32[]{:S(2)}, u32[]{:S(2)}) collective-permute-start(f32[3,1152]{1,0:T(4,128)} %get-tuple-element.8), channel_id=1, source_target_pairs={{0,1},{1,0},{2,3},{3,2},{4,5},{5,4},{6,7},{7,6},{8,9},{9,8},{10,11... | collective-permute-start | bytes 41480 | tf_op jit(solution)/shard_map/ppermute | solution.py:293
  126.4 3.8 %collective-permute-start.1 = (f32[3,1152]{1,0:T(4,128)S(1)}, f32[3,1152]{1,0:T(4,128)S(1)}, u32[]{:S(2)}, u32[]{:S(2)}) collective-permute-start(f32[3,1152]{1,0:T(4,128)S(1)} %add.12), channel_id=1, source_target_pairs={{0,2},{1,3},{2,0},{3,1},{4,6},{5,7},{6,4},{7,5},{8,10},{9,11},{10,... | collective-permute-start | bytes 41480 | tf_op jit(solution)/shard_map/ppermute | solution.py:293
  130.1 3.8 %collective-permute-start.2 = (f32[3,1152]{1,0:T(4,128)S(1)}, f32[3,1152]{1,0:T(4,128)S(1)}, u32[]{:S(2)}, u32[]{:S(2)}) collective-permute-start(f32[3,1152]{1,0:T(4,128)S(1)} %add.13), channel_id=1, source_target_pairs={{0,4},{1,5},{2,6},{3,7},{4,0},{5,1},{6,2},{7,3},{8,12},{9,13},{10,... | collective-permute-start | bytes 41480 | tf_op jit(solution)/shard_map/ppermute | solution.py:293
  133.9 4.7 %collective-permute-start.3 = (f32[3,1152]{1,0:T(4,128)S(1)}, f32[3,1152]{1,0:T(4,128)S(1)}, u32[]{:S(2)}, u32[]{:S(2)}) collective-permute-start(f32[3,1152]{1,0:T(4,128)S(1)} %add.14), channel_id=1, source_target_pairs={{0,8},{1,9},{2,10},{3,11},{4,12},{5,13},{6,14},{7,15},{8,0},{9,1},... | collective-permute-start | bytes 41480 | tf_op jit(solution)/shard_map/ppermute | solution.py:293

commit v2 on v1

--- a/solution.py
+++ b/solution.py
@@ -10,15 +10,21 @@
 
 H = 16
 LANES = 128
+STEPS = 3
+SCORE_LIMIT = 2048 * 2048
 F32 = jnp.float32
 BF16 = jnp.bfloat16
-VMEM_LIMIT = 56 * 1024 * 1024
+VMEM_LIMIT = 60 * 1024 * 1024
 
 
 def params():
     return pltpu.CompilerParams(
         dimension_semantics=("arbitrary",), vmem_limit_bytes=VMEM_LIMIT
     )
+
+
+def row(vector):
+    return vector[...].reshape(1, vector.shape[0])
 
 
 def normalise(tokens):
@@ -41,8 +47,8 @@
     @pl.when(step == 0)
     def _():
         _, normed, _ = normalise(tokens[...])
-        modulated[...] = (normed * (1.0 + scale[...]) + shift[...]).astype(BF16)
-        gated[...] = (gate[...] * cot[...].astype(F32)).astype(BF16)
+        modulated[...] = (normed * (1.0 + row(scale)) + row(shift)).astype(BF16)
+        gated[...] = (row(gate) * cot[...].astype(F32)).astype(BF16)
 
     cols = jnp.dot(modulated[...], qkv_w[...], preferred_element_type=F32)
     flat[pl.ds(pl.multiple_of(step * tile, LANES), tile), :] = cols.T
@@ -64,20 +70,20 @@
 
 def project(tokens, shift, scale, gate, qkv_w, out_w, cot):
     tok_rows, width = tokens.shape
-    steps = width // LANES
+    steps = STEPS
     head_size = width // H
-    tile = 3 * LANES
+    tile = 3 * width // steps
     whole = lambda shape: pl.BlockSpec(shape, lambda i: (0,) * len(shape))
     return pl.pallas_call(
         functools.partial(project_kernel, head_size),
         grid=(steps,),
         in_specs=[
             whole((tok_rows, width)),
-            whole((1, width)),
-            whole((1, width)),
-            whole((1, width)),
+            whole((width,)),
+            whole((width,)),
+            whole((width,)),
             pl.BlockSpec((width, tile), lambda i: (0, i)),
-            pl.BlockSpec((LANES, width), lambda i: (i, 0)),
+            pl.BlockSpec((width // steps, width), lambda i: (i, 0)),
             whole((tok_rows, width)),
         ],
         out_specs=whole((H, 4 * head_size, tok_rows)),
@@ -104,6 +110,7 @@
     chunks = items.shape[0]
     key_chunks = key_rows.shape[0] // LANES
     att_scale = 1.0 / math.sqrt(head_size)
+    exponent_scale = att_scale * math.log2(math.e)
     pad = value_rows.shape[1] - head_size
 
     @pl.when(step == 0)
@@ -127,9 +134,9 @@
     block = [items[step * group + g].astype(F32) for g in range(group)]
     queries = jnp.concatenate([b[:head_size] for b in block], axis=1)
     grads = jnp.concatenate([b[3 * head_size :] for b in block], axis=1)
-    scores = jnp.dot(key_rows[...], queries.astype(BF16), preferred_element_type=F32) * att_scale
+    scores = jnp.dot(key_rows[...], queries.astype(BF16), preferred_element_type=F32)
     row_max = jnp.max(scores, axis=0, keepdims=True)
-    exponent = jnp.exp(scores - row_max)
+    exponent = jnp.exp2((scores - row_max) * exponent_scale)
     total = jnp.sum(exponent, axis=0, keepdims=True)
     weights = (exponent * (1.0 / total)).astype(BF16)
     attended = (
@@ -176,8 +183,8 @@
     head_size = items.shape[1] // 4
     split = pairs is not None
     key_chunks = pairs.shape[0] if split else chunks
-    group = 2 if chunks % 2 == 0 else 1
     key_len = key_chunks * LANES
+    group = math.gcd(chunks, max(1, SCORE_LIMIT // (key_len * LANES)))
     pad = 8
     whole = lambda shape: pl.BlockSpec(shape, lambda i: (0,) * len(shape))
     if split:
@@ -221,8 +228,8 @@
     def _():
         flat = [items[head].astype(F32) for head in range(H)]
         att = jnp.concatenate([x[:head_size] for x in flat], axis=0)
-        for part in range(width // LANES):
-            att_cols[part] = att[part * LANES : (part + 1) * LANES, :].T.astype(BF16)
+        for part in range(width // rows):
+            att_cols[part] = att[part * rows : (part + 1) * rows, :].T.astype(BF16)
         for part in range(3):
             grad_cols[part * width : (part + 1) * width, :] = jnp.concatenate(
                 [x[(part + 1) * head_size : (part + 2) * head_size] for x in flat], axis=0
@@ -237,7 +244,7 @@
         wide, normed, inv_std = normalise(tokens[...])
         cot_wide = cot[...].astype(F32)
         out = branch[...]
-        block_output[...] = (wide + gate[...] * out).astype(BF16)
+        block_output[...] = (wide + row(gate) * out).astype(BF16)
         back = jnp.concatenate([mod_grad[i] for i in range(width // rows)], axis=1)
         sums[...] = jnp.concatenate(
             [
@@ -247,7 +254,7 @@
             ],
             axis=0,
         )
-        normed_grad = back * (1.0 + scale[...])
+        normed_grad = back * (1.0 + row(scale))
         first_mean = jnp.mean(normed_grad, axis=1, keepdims=True)
         second_mean = jnp.mean(normed_grad * normed, axis=1, keepdims=True)
         grad_input[...] = (
@@ -258,7 +265,7 @@
 def finish(items, tokens, scale, gate, qkv_w, out_w, cot):
     tok_rows, width = tokens.shape
     head_size = width // H
-    steps = width // LANES
+    steps = STEPS
     whole = lambda shape: pl.BlockSpec(shape, lambda i: (0,) * len(shape))
     return pl.pallas_call(
         functools.partial(finish_kernel, head_size),
@@ -266,10 +273,10 @@
         in_specs=[
             whole(items.shape),
             whole((tok_rows, width)),
-            whole((1, width)),
-            whole((1, width)),
-            pl.BlockSpec((LANES, 3 * width), lambda i: (i, 0)),
-            pl.BlockSpec((LANES, width), lambda i: (i, 0)),
+            whole((width,)),
+            whole((width,)),
+            pl.BlockSpec((width // steps, 3 * width), lambda i: (i, 0)),
+            pl.BlockSpec((width // steps, width), lambda i: (i, 0)),
             whole((tok_rows, width)),
         ],
         out_specs=[whole((tok_rows, width)), whole((tok_rows, width)), whole((3, width))],
@@ -279,10 +286,10 @@
             jax.ShapeDtypeStruct((3, width), F32),
         ],
         scratch_shapes=[
-            pltpu.VMEM((steps, tok_rows, LANES), BF16),
+            pltpu.VMEM((steps, tok_rows, width // steps), BF16),
             pltpu.VMEM((3 * width, tok_rows), BF16),
             pltpu.VMEM((tok_rows, width), F32),
-            pltpu.VMEM((steps, tok_rows, LANES), F32),
+            pltpu.VMEM((steps, tok_rows, width // steps), F32),
         ],
         compiler_params=params(),
         name="finish",
@@ -304,8 +311,7 @@
     tok_rows, width = tokens.shape
     head_size = width // H
     sub_rows = tok_rows // repeat
-    shift, scale, gate = (x.reshape(1, width) for x in (shift_cond, scale_cond, gate_cond))
-    packed = project(tokens, shift, scale, gate, qkv_weight, out_weight, cotangent)
+    packed = project(tokens, shift_cond, scale_cond, gate_cond, qkv_weight, out_weight, cotangent)
     if repeat == 1:
         (made,) = attend(exchange(packed))
         returned = exchange(made)
@@ -327,7 +333,7 @@
         returned = back.reshape(H, repeat, 4 * head_size, sub_rows).transpose(0, 2, 1, 3)
         returned = returned.reshape(H, 4 * head_size, tok_rows)
     block_output, grad_input, sums = finish(
-        returned, tokens, scale, gate, qkv_weight, out_weight, cotangent
+        returned, tokens, scale_cond, gate_cond, qkv_weight, out_weight, cotangent
     )
     stride = 1
     while stride < seq_count:

time: 140 us -> 120 us (0.86)
  Pallas kernels: 48.9 us -> 32.9 us
  local copies, waits for them, and re-layouts: 3.87 us -> 0 us
    pallas_call x1, Pallas kernels: 27.3 us -> 17.2 us  [attend(): pl.pallas_call(functools.partial(attend_kernel, head_size, group, split),...]
    reshape x3 -> x0, local copies, waits for them, and re-layouts: 3.87 us -> none  [per_device(): x.reshape(1, width)]
    pallas_call x1, Pallas kernels: 10.3 us -> 7.36 us  [project(): pl.pallas_call(functools.partial(project_kernel, head_size), grid=(steps,...]
    pallas_call x1, Pallas kernels: 11.3 us -> 8.34 us  [finish(): pl.pallas_call(functools.partial(finish_kernel, head_size), grid=(steps,)...]
where the time goes in v2:
time: 120 us; the launch traced here: 119 us
  blocking collectives  70.8 us (59%)
  Pallas kernels  32.9 us (27%)
  waiting for transfers between devices  10.4 us (9%)
  starting transfers between devices  3.21 us (3%)
  other arithmetic  1.35 us (1%)
    all_to_all x2, blocking collectives, exchange(): lax.all_to_all(blocks, 'seq', split_axis=0, concat_axis=0, tiled=True)  70.8 us
    pallas_call x1, Pallas kernels, attend(): pl.pallas_call(functools.partial(attend_kernel, head_size, group, split),...  17.2 us
    ppermute x4, waiting for transfers between devices, from_partner(): lax.ppermute(shard, axis, [(i, i ^ stride) for i in range(lax.axis_size(a...  10.4 us
    pallas_call x1, Pallas kernels, finish(): pl.pallas_call(functools.partial(finish_kernel, head_size), grid=(steps,)...  8.34 us
    pallas_call x1, Pallas kernels, project(): pl.pallas_call(functools.partial(project_kernel, head_size), grid=(steps,...  7.36 us
    ppermute x4, starting transfers between devices, from_partner(): lax.ppermute(shard, axis, [(i, i ^ stride) for i in range(lax.axis_size(a...  3.21 us
  transfers between devices with their start and end apart: 4, of which 4 were waited for; matrix products, arithmetic and copies ran while one was open for 0% of the time, Pallas kernels for 0%

profile of v2, /device:TPU:0, one launch (start us, length us, event | category | flops | bytes accessed | tf_op | source)
XLA Modules:
  0.0 119.2 jit_solution(9403471164081782804)
XLA Ops:
  0.6 7.4 %project.1 = bf16[16,288,128]{2,1,0:T(8,128)(2,1)} custom-call(bf16[128,1152]{1,0:T(8,128)(2,1)} %tokens.3, f32[1152]{0:T(1024)} %shift.1, f32[1152]{0:T(1024)} %scale.3, f32[1152]{0:T(1024)} %gate.3, bf16[1152,3456]{1,0:T(8,128)(2,1)} %qkv_w.3, bf16[1152,1152]{1,0:T(8,128)(2,1)} %out_w.3, bf16[128,1152]{1,0:T(8,128)(2,1)} %cot.3), custom_call_target="tpu_custom_call" | custom-call | tf_op jit(solution)/shard_map/project/pallas_call | solution.py:77
  8.0 37.0 %all_to_all.10.items = bf16[16,288,128]{2,1,0:T(8,128)(2,1)} all-to-all(bf16[16,288,128]{2,1,0:T(8,128)(2,1)} %project.1), channel_id=1, replica_groups=mesh['groups'=2,'seq'=16] {'seq'}, dimensions={0} | all-to-all | bytes 2359296 | tf_op jit(solution)/shard_map/all_to_all | solution.py:304
  45.0 17.2 %attend.1 = bf16[16,288,128]{2,1,0:T(8,128)(2,1)} custom-call(bf16[16,288,128]{2,1,0:T(8,128)(2,1)} %all_to_all.10.items), custom_call_target="tpu_custom_call" | custom-call | tf_op jit(solution)/shard_map/attend/pallas_call | solution.py:199
  62.1 33.8 %all_to_all.11.items = bf16[16,288,128]{2,1,0:T(8,128)(2,1)} all-to-all(bf16[16,288,128]{2,1,0:T(8,128)(2,1)} %attend.1), channel_id=1, replica_groups=mesh['groups'=2,'seq'=16] {'seq'}, dimensions={0} | all-to-all | bytes 2359296 | tf_op jit(solution)/shard_map/all_to_all | solution.py:304
  96.0 8.3 %finish.1 = (bf16[128,1152]{1,0:T(8,128)(2,1)}, bf16[128,1152]{1,0:T(8,128)(2,1)}, f32[3,1152]{1,0:T(4,128)}) custom-call(bf16[16,288,128]{2,1,0:T(8,128)(2,1)} %all_to_all.11.items, bf16[128,1152]{1,0:T(8,128)(2,1)} %tokens.3, f32[1152]{0:T(1024)} %scale.3, f32[1152]{0:T(1024)} %gate.3, bf16[1152,3456]{1,0:T(8,128)(2,1)} %qkv_w.3, ...), custom_call_target="tpu_custom_call" | custom-call | tf_op jit(solution)/shard_map/finish/pallas_call | solution.py:270
  104.3 0.3 collective-permute-start
  104.6 1.1 collective-permute-done
  105.7 0.7 add.12
  106.4 0.7 collective-permute-start.1
  107.2 3.0 %collective-permute-done.1 = f32[3,1152]{1,0:T(4,128)S(1)} collective-permute-done((f32[3,1152]{1,0:T(4,128)S(1)}, f32[3,1152]{1,0:T(4,128)S(1)}, u32[]{:S(2)}, u32[]{:S(2)}) %collective-permute-start.1) | collective-permute-done | bytes 13856 | tf_op jit(solution)/shard_map/ppermute | solution.py:300
  110.2 0.9 collective-permute-start.2
  111.1 2.9 %collective-permute-done.2 = f32[3,1152]{1,0:T(4,128)S(1)} collective-permute-done((f32[3,1152]{1,0:T(4,128)S(1)}, f32[3,1152]{1,0:T(4,128)S(1)}, u32[]{:S(2)}, u32[]{:S(2)}) %collective-permute-start.2) | collective-permute-done | bytes 13856 | tf_op jit(solution)/shard_map/ppermute | solution.py:300
  114.0 1.3 %collective-permute-start.3 = (f32[3,1152]{1,0:T(4,128)S(1)}, f32[3,1152]{1,0:T(4,128)S(1)}, u32[]{:S(2)}, u32[]{:S(2)}) collective-permute-start(f32[3,1152]{1,0:T(4,128)S(1)} %add.14), channel_id=1, source_target_pairs={{0,8},{1,9},{2,10},{3,11},{4,12},{5,13},{6,14},{7,15},{8,0},{9,1},... | collective-permute-start | bytes 41480 | tf_op jit(solution)/shard_map/ppermute | solution.py:300
  115.2 3.4 %collective-permute-done.3 = f32[3,1152]{1,0:T(4,128)S(1)} collective-permute-done((f32[3,1152]{1,0:T(4,128)S(1)}, f32[3,1152]{1,0:T(4,128)S(1)}, u32[]{:S(2)}, u32[]{:S(2)}) %collective-permute-start.3) | collective-permute-done | bytes 13856 | tf_op jit(solution)/shard_map/ppermute | solution.py:300
  118.6 0.6 add_multiply_fusion
  (2 shorter events, 0.0 us)
Async XLA Ops:
  104.3 1.4 %collective-permute-start = (f32[3,1152]{1,0:T(4,128)}, f32[3,1152]{1,0:T(4,128)S(1)}, u32[]{:S(2)}, u32[]{:S(2)}) collective-permute-start(f32[3,1152]{1,0:T(4,128)} %get-tuple-element.8), channel_id=1, source_target_pairs={{0,1},{1,0},{2,3},{3,2},{4,5},{5,4},{6,7},{7,6},{8,9},{9,8},{10,11... | collective-permute-start | bytes 41480 | tf_op jit(solution)/shard_map/ppermute | solution.py:300
  106.4 3.8 %collective-permute-start.1 = (f32[3,1152]{1,0:T(4,128)S(1)}, f32[3,1152]{1,0:T(4,128)S(1)}, u32[]{:S(2)}, u32[]{:S(2)}) collective-permute-start(f32[3,1152]{1,0:T(4,128)S(1)} %add.12), channel_id=1, source_target_pairs={{0,2},{1,3},{2,0},{3,1},{4,6},{5,7},{6,4},{7,5},{8,10},{9,11},{10,... | collective-permute-start | bytes 41480 | tf_op jit(solution)/shard_map/ppermute | solution.py:300
  110.2 3.8 %collective-permute-start.2 = (f32[3,1152]{1,0:T(4,128)S(1)}, f32[3,1152]{1,0:T(4,128)S(1)}, u32[]{:S(2)}, u32[]{:S(2)}) collective-permute-start(f32[3,1152]{1,0:T(4,128)S(1)} %add.13), channel_id=1, source_target_pairs={{0,4},{1,5},{2,6},{3,7},{4,0},{5,1},{6,2},{7,3},{8,12},{9,13},{10,... | collective-permute-start | bytes 41480 | tf_op jit(solution)/shard_map/ppermute | solution.py:300
  114.0 4.7 %collective-permute-start.3 = (f32[3,1152]{1,0:T(4,128)S(1)}, f32[3,1152]{1,0:T(4,128)S(1)}, u32[]{:S(2)}, u32[]{:S(2)}) collective-permute-start(f32[3,1152]{1,0:T(4,128)S(1)} %add.14), channel_id=1, source_target_pairs={{0,8},{1,9},{2,10},{3,11},{4,12},{5,13},{6,14},{7,15},{8,0},{9,1},... | collective-permute-start | bytes 41480 | tf_op jit(solution)/shard_map/ppermute | solution.py:300

commit v3 on v2

--- a/solution.py
+++ b/solution.py
@@ -14,13 +14,13 @@
 SCORE_LIMIT = 2048 * 2048
 F32 = jnp.float32
 BF16 = jnp.bfloat16
-VMEM_LIMIT = 60 * 1024 * 1024
-
-
-def params():
-    return pltpu.CompilerParams(
-        dimension_semantics=("arbitrary",), vmem_limit_bytes=VMEM_LIMIT
-    )
+PROJECT_LIMIT = 60 * 1024 * 1024
+ATTEND_LIMIT = 44 * 1024 * 1024
+FINISH_LIMIT = 24 * 1024 * 1024
+
+
+def params(limit):
+    return pltpu.CompilerParams(dimension_semantics=("arbitrary",), vmem_limit_bytes=limit)
 
 
 def row(vector):
@@ -93,20 +93,21 @@
             pltpu.VMEM((tok_rows, width), BF16),
             pltpu.VMEM((4 * width, tok_rows), F32),
         ],
-        compiler_params=params(),
+        compiler_params=params(PROJECT_LIMIT),
         name="project",
     )(tokens, shift, scale, gate, qkv_w, out_w, cot)
 
 
-def attend_kernel(head_size, group, split, items, *refs):
+def attend_kernel(head_size, group, split, items, weight, *refs):
     if split:
-        pairs, near, far = refs[:3]
-        refs = refs[3:]
+        pairs, held, near, far = refs[:4]
+        refs = refs[4:]
     else:
-        near = refs[0]
-        refs = refs[1:]
-    key_rows, value_rows, key_cols, value_cols, key_grad, value_grad, near_flat = refs
+        held, near = refs[:2]
+        refs = refs[2:]
+    key_rows, value_rows, key_cols, value_cols, key_grad, value_grad, near_flat, sem = refs
     step = pl.program_id(0)
+    load = pltpu.make_async_copy(weight, held, sem)
     chunks = items.shape[0]
     key_chunks = key_rows.shape[0] // LANES
     att_scale = 1.0 / math.sqrt(head_size)
@@ -115,6 +116,7 @@
 
     @pl.when(step == 0)
     def _():
+        load.start()
         for s in range(key_chunks):
             if split:
                 pair = pairs[s].astype(F32)
@@ -176,9 +178,10 @@
                 near[s] = jnp.concatenate([near_flat[s], grads_of], axis=0).astype(BF16)
         if split:
             near[...] = near_flat[...].astype(BF16)
-
-
-def attend(items, pairs=None):
+        load.wait()
+
+
+def attend(items, weight, pairs=None):
     chunks = items.shape[0]
     head_size = items.shape[1] // 4
     split = pairs is not None
@@ -192,15 +195,18 @@
             jax.ShapeDtypeStruct((chunks, 2 * head_size, LANES), BF16),
             jax.ShapeDtypeStruct((key_chunks, 2 * head_size, LANES), F32),
         ]
-        operands = (items, pairs)
+        operands = (items, weight, pairs)
     else:
         shapes = [jax.ShapeDtypeStruct((chunks, 4 * head_size, LANES), BF16)]
-        operands = (items,)
+        operands = (items, weight)
+    specs = [whole(x.shape) for x in operands]
+    specs[1] = pl.BlockSpec(memory_space=pl.ANY)
+    shapes = [jax.ShapeDtypeStruct(weight.shape, weight.dtype)] + shapes
     return pl.pallas_call(
         functools.partial(attend_kernel, head_size, group, split),
         grid=(chunks // group,),
-        in_specs=[whole(x.shape) for x in operands],
-        out_specs=[whole(x.shape) for x in shapes],
+        in_specs=specs,
+        out_specs=[pl.BlockSpec(memory_space=pltpu.VMEM)] + [whole(x.shape) for x in shapes[1:]],
         out_shape=shapes,
         scratch_shapes=[
             pltpu.VMEM((key_len, head_size), BF16),
@@ -210,88 +216,60 @@
             pltpu.VMEM((key_len, head_size), F32),
             pltpu.VMEM((key_len, head_size), F32),
             pltpu.VMEM((chunks, 2 * head_size, LANES), F32),
-        ],
-        compiler_params=params(),
+            pltpu.SemaphoreType.DMA,
+        ],
+        compiler_params=params(ATTEND_LIMIT),
         name="attend",
     )(*operands)
 
 
 def finish_kernel(
     head_size, items, tokens, scale, gate, qkv_w, out_w, cot,
-    block_output, grad_input, sums, att_cols, grad_cols, branch, mod_grad,
+    block_output, grad_input, sums, grad_cols,
 ):
-    step = pl.program_id(0)
     width = tokens.shape[1]
-    rows = qkv_w.shape[0]
-
-    @pl.when(step == 0)
-    def _():
-        flat = [items[head].astype(F32) for head in range(H)]
-        att = jnp.concatenate([x[:head_size] for x in flat], axis=0)
-        for part in range(width // rows):
-            att_cols[part] = att[part * rows : (part + 1) * rows, :].T.astype(BF16)
-        for part in range(3):
-            grad_cols[part * width : (part + 1) * width, :] = jnp.concatenate(
-                [x[(part + 1) * head_size : (part + 2) * head_size] for x in flat], axis=0
-            ).astype(BF16)
-        branch[...] = jnp.zeros_like(branch)
-
-    branch[...] += jnp.dot(att_cols[step], out_w[...], preferred_element_type=F32)
-    mod_grad[step] = jnp.dot(qkv_w[...], grad_cols[...], preferred_element_type=F32).T
-
-    @pl.when(step == pl.num_programs(0) - 1)
-    def _():
-        wide, normed, inv_std = normalise(tokens[...])
-        cot_wide = cot[...].astype(F32)
-        out = branch[...]
-        block_output[...] = (wide + row(gate) * out).astype(BF16)
-        back = jnp.concatenate([mod_grad[i] for i in range(width // rows)], axis=1)
-        sums[...] = jnp.concatenate(
-            [
-                jnp.sum(back, axis=0, keepdims=True),
-                jnp.sum(back * normed, axis=0, keepdims=True),
-                jnp.sum(cot_wide * out, axis=0, keepdims=True),
-            ],
-            axis=0,
-        )
-        normed_grad = back * (1.0 + row(scale))
-        first_mean = jnp.mean(normed_grad, axis=1, keepdims=True)
-        second_mean = jnp.mean(normed_grad * normed, axis=1, keepdims=True)
-        grad_input[...] = (
-            cot_wide + inv_std * (normed_grad - first_mean - normed * second_mean)
+    flat = [items[head].astype(F32) for head in range(H)]
+    for part in range(3):
+        grad_cols[part * width : (part + 1) * width, :] = jnp.concatenate(
+            [x[(part + 1) * head_size : (part + 2) * head_size] for x in flat], axis=0
         ).astype(BF16)
+    att = jnp.concatenate([x[:head_size] for x in flat], axis=0).T.astype(BF16)
+    out = jnp.dot(att, out_w[...], preferred_element_type=F32)
+    back = jnp.dot(qkv_w[...], grad_cols[...], preferred_element_type=F32).T
+    wide, normed, inv_std = normalise(tokens[...])
+    cot_wide = cot[...].astype(F32)
+    block_output[...] = (wide + row(gate) * out).astype(BF16)
+    sums[...] = jnp.concatenate(
+        [
+            jnp.sum(back, axis=0, keepdims=True),
+            jnp.sum(back * normed, axis=0, keepdims=True),
+            jnp.sum(cot_wide * out, axis=0, keepdims=True),
+        ],
+        axis=0,
+    )
+    normed_grad = back * (1.0 + row(scale))
+    first_mean = jnp.mean(normed_grad, axis=1, keepdims=True)
+    second_mean = jnp.mean(normed_grad * normed, axis=1, keepdims=True)
+    grad_input[...] = (
+        cot_wide + inv_std * (normed_grad - first_mean - normed * second_mean)
+    ).astype(BF16)
 
 
 def finish(items, tokens, scale, gate, qkv_w, out_w, cot):
     tok_rows, width = tokens.shape
     head_size = width // H
-    steps = STEPS
-    whole = lambda shape: pl.BlockSpec(shape, lambda i: (0,) * len(shape))
+    vmem = pl.BlockSpec(memory_space=pltpu.VMEM)
     return pl.pallas_call(
         functools.partial(finish_kernel, head_size),
-        grid=(steps,),
-        in_specs=[
-            whole(items.shape),
-            whole((tok_rows, width)),
-            whole((width,)),
-            whole((width,)),
-            pl.BlockSpec((width // steps, 3 * width), lambda i: (i, 0)),
-            pl.BlockSpec((width // steps, width), lambda i: (i, 0)),
-            whole((tok_rows, width)),
-        ],
-        out_specs=[whole((tok_rows, width)), whole((tok_rows, width)), whole((3, width))],
+        in_specs=[vmem] * 7,
+        out_specs=[vmem] * 3,
         out_shape=[
             jax.ShapeDtypeStruct((tok_rows, width), BF16),
             jax.ShapeDtypeStruct((tok_rows, width), BF16),
             jax.ShapeDtypeStruct((3, width), F32),
         ],
-        scratch_shapes=[
-            pltpu.VMEM((steps, tok_rows, width // steps), BF16),
-            pltpu.VMEM((3 * width, tok_rows), BF16),
-            pltpu.VMEM((tok_rows, width), F32),
-            pltpu.VMEM((steps, tok_rows, width // steps), F32),
-        ],
-        compiler_params=params(),
+        scratch_shapes=[pltpu.VMEM((3 * width, tok_rows), BF16)],
+        compiler_params=pltpu.CompilerParams(vmem_limit_bytes=FINISH_LIMIT),
         name="finish",
     )(items, tokens, scale, gate, qkv_w, out_w, cot)
 
@@ -313,7 +291,7 @@
     sub_rows = tok_rows // repeat
     packed = project(tokens, shift_cond, scale_cond, gate_cond, qkv_weight, out_weight, cotangent)
     if repeat == 1:
-        (made,) = attend(exchange(packed))
+        held, made = attend(exchange(packed), qkv_weight)
         returned = exchange(made)
     else:
         packed = packed.reshape(H, 4 * head_size, repeat, sub_rows).transpose(0, 2, 1, 3)
@@ -323,7 +301,7 @@
         pairs = items[:, head_size : 3 * head_size]
         for level in range(levels):
             pairs = jnp.concatenate([pairs, from_partner(pairs, "seq", 1 << level)], axis=0)
-        near, far = attend(items, pairs)
+        held, near, far = attend(items, qkv_weight, pairs)
         for level in reversed(range(levels)):
             middle = far.shape[0] // 2
             far = far[:middle] + from_partner(far[middle:], "seq", 1 << level)
@@ -333,7 +311,7 @@
         returned = back.reshape(H, repeat, 4 * head_size, sub_rows).transpose(0, 2, 1, 3)
         returned = returned.reshape(H, 4 * head_size, tok_rows)
     block_output, grad_input, sums = finish(
-        returned, tokens, scale_cond, gate_cond, qkv_weight, out_weight, cotangent
+        returned, tokens, scale_cond, gate_cond, held, out_weight, cotangent
     )
     stride = 1
     while stride < seq_count:

time: 120 us -> 111 us (0.925)
  Pallas kernels: 32.9 us -> 26.2 us
  blocking collectives: 70.8 us -> 69.6 us
    pallas_call x1, Pallas kernels: 8.34 us -> 3.94 us  [finish(): pl.pallas_call(functools.partial(finish_kernel, head_size), in_specs=[vme...]
    pallas_call x1, Pallas kernels: 17.2 us -> 14.9 us  [attend(): pl.pallas_call(functools.partial(attend_kernel, head_size, group, split),...]
    all_to_all x2, blocking collectives: 70.8 us -> 69.6 us  [exchange(): lax.all_to_all(blocks, 'seq', split_axis=0, concat_axis=0, tiled=True)]
where the time goes in v3:
time: 111 us; the launch traced here: 110 us
  blocking collectives  69.6 us (63%)
  Pallas kernels  26.2 us (24%)
  waiting for transfers between devices  10.1 us (9%)
  starting transfers between devices  3.25 us (3%)
    all_to_all x2, blocking collectives, exchange(): lax.all_to_all(blocks, 'seq', split_axis=0, concat_axis=0, tiled=True)  69.6 us
    pallas_call x1, Pallas kernels, attend(): pl.pallas_call(functools.partial(attend_kernel, head_size, group, split),...  14.9 us
    ppermute x4, waiting for transfers between devices, from_partner(): lax.ppermute(shard, axis, [(i, i ^ stride) for i in range(lax.axis_size(a...  10.1 us
    pallas_call x1, Pallas kernels, project(): pl.pallas_call(functools.partial(project_kernel, head_size), grid=(steps,...  7.35 us
    pallas_call x1, Pallas kernels, finish(): pl.pallas_call(functools.partial(finish_kernel, head_size), in_specs=[vme...  3.94 us
    ppermute x4, starting transfers between devices, from_partner(): lax.ppermute(shard, axis, [(i, i ^ stride) for i in range(lax.axis_size(a...  3.25 us
  transfers between devices with their start and end apart: 4, of which 4 were waited for; matrix products, arithmetic and copies ran while one was open for 0% of the time, Pallas kernels for 0%

profile of v3, /device:TPU:0, one launch (start us, length us, event | category | flops | bytes accessed | tf_op | source)
XLA Modules:
  0.0 110.5 jit_solution(4022249331239347516)
XLA Ops:
  0.6 7.4 %project.1 = bf16[16,288,128]{2,1,0:T(8,128)(2,1)} custom-call(bf16[128,1152]{1,0:T(8,128)(2,1)} %tokens.3, f32[1152]{0:T(1024)} %shift.1, f32[1152]{0:T(1024)} %scale.3, f32[1152]{0:T(1024)} %gate.3, bf16[1152,3456]{1,0:T(8,128)(2,1)} %weight.1, bf16[1152,1152]{1,0:T(8,128)(2,1)} %out_w.3, bf16[128,1152]{1,0:T(8,128)(2,1)} %cot.3), custom_call_target="tpu_custom_call" | custom-call | tf_op jit(solution)/shard_map/project/pallas_call | solution.py:77
  8.0 36.9 %all_to_all.10.items = bf16[16,288,128]{2,1,0:T(8,128)(2,1)S(1)} all-to-all(bf16[16,288,128]{2,1,0:T(8,128)(2,1)} %project.1), channel_id=1, replica_groups=mesh['groups'=2,'seq'=16] {'seq'}, dimensions={0} | all-to-all | bytes 2359296 | tf_op jit(solution)/shard_map/all_to_all | solution.py:282
  44.9 0.0 copy-start
  44.9 14.9 %attend.1 = (bf16[1152,3456]{1,0:T(8,128)(2,1)S(1)}, bf16[16,288,128]{2,1,0:T(8,128)(2,1)S(1)}) custom-call(bf16[16,288,128]{2,1,0:T(8,128)(2,1)S(1)} %all_to_all.10.items, bf16[1152,3456]{1,0:T(8,128)(2,1)} %weight.1), custom_call_target="tpu_custom_call" | custom-call | tf_op jit(solution)/shard_map/attend/pallas_call | solution.py:205
  59.7 0.0 copy-start.1
  59.8 0.0 copy-start.2
  59.8 0.0 copy-start.3
  59.8 0.0 copy-start.4
  59.8 32.7 %all_to_all.11.items = bf16[16,288,128]{2,1,0:T(8,128)(2,1)S(1)} all-to-all(bf16[16,288,128]{2,1,0:T(8,128)(2,1)S(1)} %get-tuple-element.8), channel_id=1, replica_groups=mesh['groups'=2,'seq'=16] {'seq'}, dimensions={0} | all-to-all | bytes 2359296 | tf_op jit(solution)/shard_map/all_to_all | solution.py:282
  92.5 0.0 copy-done
  92.5 0.0 copy-done.1
  92.5 0.0 copy-done.2
  92.5 0.0 copy-done.3
  92.5 0.0 copy-done.4
  92.5 3.9 %finish.1 = (bf16[128,1152]{1,0:T(8,128)(2,1)}, bf16[128,1152]{1,0:T(8,128)(2,1)}, f32[3,1152]{1,0:T(4,128)S(1)}) custom-call(bf16[16,288,128]{2,1,0:T(8,128)(2,1)S(1)} %all_to_all.11.items, bf16[128,1152]{1,0:T(8,128)(2,1)S(1)} %copy-done.1, f32[1152]{0:T(1024)S(1)} %copy-done.3, f32[1152]{0:T(1024)S(1)} %copy-done.4, ...), custom_call_target="tpu_custom_call" | custom-call | tf_op jit(solution)/shard_map/finish/pallas_call | solution.py:262
  96.5 0.3 collective-permute-start
  96.8 0.9 collective-permute-done
  97.7 0.7 collective-permute-start.1
  98.4 3.0 %collective-permute-done.1 = f32[3,1152]{1,0:T(4,128)S(1)} collective-permute-done((f32[3,1152]{1,0:T(4,128)S(1)}, f32[3,1152]{1,0:T(4,128)S(1)}, u32[]{:S(2)}, u32[]{:S(2)}) %collective-permute-start.1) | collective-permute-done | bytes 13856 | tf_op jit(solution)/shard_map/ppermute | solution.py:278
  101.4 0.9 collective-permute-start.2
  102.3 2.9 %collective-permute-done.2 = f32[3,1152]{1,0:T(4,128)S(1)} collective-permute-done((f32[3,1152]{1,0:T(4,128)S(1)}, f32[3,1152]{1,0:T(4,128)S(1)}, u32[]{:S(2)}, u32[]{:S(2)}) %collective-permute-start.2) | collective-permute-done | bytes 13856 | tf_op jit(solution)/shard_map/ppermute | solution.py:278
  105.2 1.3 %collective-permute-start.3 = (f32[3,1152]{1,0:T(4,128)S(1)}, f32[3,1152]{1,0:T(4,128)S(1)}, u32[]{:S(2)}, u32[]{:S(2)}) collective-permute-start(f32[3,1152]{1,0:T(4,128)S(1)} %add.14), channel_id=1, source_target_pairs={{0,8},{1,9},{2,10},{3,11},{4,12},{5,13},{6,14},{7,15},{8,0},{9,1},... | collective-permute-start | bytes 41480 | tf_op jit(solution)/shard_map/ppermute | solution.py:278
  106.5 3.4 %collective-permute-done.3 = f32[3,1152]{1,0:T(4,128)S(1)} collective-permute-done((f32[3,1152]{1,0:T(4,128)S(1)}, f32[3,1152]{1,0:T(4,128)S(1)}, u32[]{:S(2)}, u32[]{:S(2)}) %collective-permute-start.3) | collective-permute-done | bytes 13856 | tf_op jit(solution)/shard_map/ppermute | solution.py:278
  109.9 0.6 add_multiply_fusion
  (3 shorter events, 0.0 us)
Async XLA Ops:
  44.9 47.7 %copy-start = (bf16[1152,1152]{1,0:T(8,128)(2,1)S(1)}, bf16[1152,1152]{1,0:T(8,128)(2,1)}, u32[]{:S(2)}) copy-start(bf16[1152,1152]{1,0:T(8,128)(2,1)} %out_w.3) | copy-start | bytes 7962628
  59.7 32.8 %copy-start.1 = (bf16[128,1152]{1,0:T(8,128)(2,1)S(1)}, bf16[128,1152]{1,0:T(8,128)(2,1)}, u32[]{:S(2)}) copy-start(bf16[128,1152]{1,0:T(8,128)(2,1)} %tokens.3) | copy-start | bytes 884740
  59.8 32.8 %copy-start.2 = (bf16[128,1152]{1,0:T(8,128)(2,1)S(1)}, bf16[128,1152]{1,0:T(8,128)(2,1)}, u32[]{:S(2)}) copy-start(bf16[128,1152]{1,0:T(8,128)(2,1)} %cot.3) | copy-start | bytes 884740
  59.8 32.7 %copy-start.3 = (f32[1152]{0:T(1024)S(1)}, f32[1152]{0:T(1024)}, u32[]{:S(2)}) copy-start(f32[1152]{0:T(1024)} %scale.3) | copy-start | bytes 13828
  59.8 32.7 %copy-start.4 = (f32[1152]{0:T(1024)S(1)}, f32[1152]{0:T(1024)}, u32[]{:S(2)}) copy-start(f32[1152]{0:T(1024)} %gate.3) | copy-start | bytes 13828
  96.5 1.2 %collective-permute-start = (f32[3,1152]{1,0:T(4,128)S(1)}, f32[3,1152]{1,0:T(4,128)S(1)}, u32[]{:S(2)}, u32[]{:S(2)}) collective-permute-start(f32[3,1152]{1,0:T(4,128)S(1)} %get-tuple-element.12), channel_id=1, source_target_pairs={{0,1},{1,0},{2,3},{3,2},{4,5},{5,4},{6,7},{7,6},{8,9},{9,8},{10,11... | collective-permute-start | bytes 41480 | tf_op jit(solution)/shard_map/ppermute | solution.py:278
  97.7 3.8 %collective-permute-start.1 = (f32[3,1152]{1,0:T(4,128)S(1)}, f32[3,1152]{1,0:T(4,128)S(1)}, u32[]{:S(2)}, u32[]{:S(2)}) collective-permute-start(f32[3,1152]{1,0:T(4,128)S(1)} %add.12), channel_id=1, source_target_pairs={{0,2},{1,3},{2,0},{3,1},{4,6},{5,7},{6,4},{7,5},{8,10},{9,11},{10,... | collective-permute-start | bytes 41480 | tf_op jit(solution)/shard_map/ppermute | solution.py:278
  101.4 3.8 %collective-permute-start.2 = (f32[3,1152]{1,0:T(4,128)S(1)}, f32[3,1152]{1,0:T(4,128)S(1)}, u32[]{:S(2)}, u32[]{:S(2)}) collective-permute-start(f32[3,1152]{1,0:T(4,128)S(1)} %add.13), channel_id=1, source_target_pairs={{0,4},{1,5},{2,6},{3,7},{4,0},{5,1},{6,2},{7,3},{8,12},{9,13},{10,... | collective-permute-start | bytes 41480 | tf_op jit(solution)/shard_map/ppermute | solution.py:278
  105.2 4.7 %collective-permute-start.3 = (f32[3,1152]{1,0:T(4,128)S(1)}, f32[3,1152]{1,0:T(4,128)S(1)}, u32[]{:S(2)}, u32[]{:S(2)}) collective-permute-start(f32[3,1152]{1,0:T(4,128)S(1)} %add.14), channel_id=1, source_target_pairs={{0,8},{1,9},{2,10},{3,11},{4,12},{5,13},{6,14},{7,15},{8,0},{9,1},... | collective-permute-start | bytes 41480 | tf_op jit(solution)/shard_map/ppermute | solution.py:278

commit v4 on v3

--- a/solution.py
+++ b/solution.py
@@ -10,7 +10,6 @@
 
 H = 16
 LANES = 128
-STEPS = 3
 SCORE_LIMIT = 2048 * 2048
 F32 = jnp.float32
 BF16 = jnp.bfloat16
@@ -36,66 +35,66 @@
     return wide, centered * inv_std, inv_std
 
 
-def project_kernel(
-    head_size, tokens, shift, scale, gate, qkv_w, out_w, cot, packed, modulated, gated, flat
-):
-    step = pl.program_id(0)
+def project_kernel(head_size, *refs):
+    sources, out, held, sems, packed = refs[:7], refs[7], refs[8:15], refs[15], refs[16]
+    tokens, shift, scale, gate, cot, out_w, qkv_w = held
     width = tokens.shape[1]
-    tile = qkv_w.shape[1]
-    rows = out_w.shape[0]
-
-    @pl.when(step == 0)
-    def _():
-        _, normed, _ = normalise(tokens[...])
-        modulated[...] = (normed * (1.0 + row(scale)) + row(shift)).astype(BF16)
-        gated[...] = (row(gate) * cot[...].astype(F32)).astype(BF16)
-
-    cols = jnp.dot(modulated[...], qkv_w[...], preferred_element_type=F32)
-    flat[pl.ds(pl.multiple_of(step * tile, LANES), tile), :] = cols.T
-    flat[pl.ds(pl.multiple_of(3 * width + step * rows, LANES), rows), :] = lax.dot_general(
-        out_w[...], gated[...], (((1,), (1,)), ((), ())), preferred_element_type=F32
-    )
-
-    @pl.when(step == pl.num_programs(0) - 1)
-    def _():
+    copies = [
+        pltpu.make_async_copy(source, target, sems.at[i])
+        for i, (source, target) in enumerate(zip(sources[:6], held[:6]))
+    ]
+    parts = [slice(part * width, (part + 1) * width) for part in range(3)]
+    copies += [
+        pltpu.make_async_copy(sources[6].at[:, at], qkv_w.at[:, at], sems.at[6 + part])
+        for part, at in enumerate(parts)
+    ]
+    for copy in copies:
+        copy.start()
+    for copy in copies[:5]:
+        copy.wait()
+    _, normed, _ = normalise(tokens[...])
+    modulated = (normed * (1.0 + row(scale)) + row(shift)).astype(BF16)
+    gated = (row(gate) * cot[...].astype(F32)).astype(BF16)
+    copies[5].wait()
+    pulled = lax.dot_general(
+        out_w[...], gated, (((1,), (1,)), ((), ())), preferred_element_type=F32
+    )
+
+    def part_of(part):
+        copies[6 + part].wait()
+        return jnp.dot(modulated, qkv_w[:, parts[part]], preferred_element_type=F32).T
+
+    def send(first, second, half):
+        rows = slice(half * 2 * head_size, (half + 1) * 2 * head_size)
         for head in range(H):
-            packed[head] = jnp.concatenate(
-                [
-                    flat[part * width + head * head_size : part * width + (head + 1) * head_size, :]
-                    for part in range(4)
-                ],
-                axis=0,
-            ).astype(BF16)
+            at = slice(head * head_size, (head + 1) * head_size)
+            packed[head, rows, :] = jnp.concatenate([first[at], second[at]], axis=0).astype(BF16)
+        copy = pltpu.make_async_copy(packed.at[:, rows, :], out.at[:, rows, :], sems.at[9 + half])
+        copy.start()
+        return copy
+
+    leaving = [send(part_of(0), part_of(1), 0)]
+    leaving.append(send(part_of(2), pulled, 1))
+    for copy in leaving:
+        copy.wait()
 
 
 def project(tokens, shift, scale, gate, qkv_w, out_w, cot):
     tok_rows, width = tokens.shape
-    steps = STEPS
     head_size = width // H
-    tile = 3 * width // steps
-    whole = lambda shape: pl.BlockSpec(shape, lambda i: (0,) * len(shape))
+    operands = (tokens, shift, scale, gate, cot, out_w, qkv_w)
+    hbm = pl.BlockSpec(memory_space=pl.ANY)
+    packed = (H, 4 * head_size, tok_rows)
     return pl.pallas_call(
         functools.partial(project_kernel, head_size),
-        grid=(steps,),
-        in_specs=[
-            whole((tok_rows, width)),
-            whole((width,)),
-            whole((width,)),
-            whole((width,)),
-            pl.BlockSpec((width, tile), lambda i: (0, i)),
-            pl.BlockSpec((width // steps, width), lambda i: (i, 0)),
-            whole((tok_rows, width)),
-        ],
-        out_specs=whole((H, 4 * head_size, tok_rows)),
-        out_shape=jax.ShapeDtypeStruct((H, 4 * head_size, tok_rows), BF16),
-        scratch_shapes=[
-            pltpu.VMEM((tok_rows, width), BF16),
-            pltpu.VMEM((tok_rows, width), BF16),
-            pltpu.VMEM((4 * width, tok_rows), F32),
-        ],
-        compiler_params=params(PROJECT_LIMIT),
+        in_specs=[hbm] * 7,
+        out_specs=hbm,
+        out_shape=jax.ShapeDtypeStruct(packed, BF16),
+        scratch_shapes=[pltpu.VMEM(x.shape, x.dtype) for x in operands]
+        + [pltpu.SemaphoreType.DMA((11,)), pltpu.VMEM(packed, BF16)],
+        compiler_params=pltpu.CompilerParams(vmem_limit_bytes=PROJECT_LIMIT),
         name="project",
-    )(tokens, shift, scale, gate, qkv_w, out_w, cot)
+    )(*operands)
 
 
 def attend_kernel(head_size, group, split, items, weight, *refs):
@@ -223,9 +222,8 @@
     )(*operands)
 
 
-def finish_kernel(
-    head_size, items, tokens, scale, gate, qkv_w, out_w, cot,
-    block_output, grad_input, sums, grad_cols,
+def gather_kernel(
+    head_size, items, tokens, qkv_w, out_w, cot, branch, mod_grad, sums, grad_cols
 ):
     width = tokens.shape[1]
     flat = [items[head].astype(F32) for head in range(H)]
@@ -236,42 +234,61 @@
     att = jnp.concatenate([x[:head_size] for x in flat], axis=0).T.astype(BF16)
     out = jnp.dot(att, out_w[...], preferred_element_type=F32)
     back = jnp.dot(qkv_w[...], grad_cols[...], preferred_element_type=F32).T
-    wide, normed, inv_std = normalise(tokens[...])
-    cot_wide = cot[...].astype(F32)
-    block_output[...] = (wide + row(gate) * out).astype(BF16)
+    _, normed, _ = normalise(tokens[...])
+    branch[...] = out
+    mod_grad[...] = back
     sums[...] = jnp.concatenate(
         [
             jnp.sum(back, axis=0, keepdims=True),
             jnp.sum(back * normed, axis=0, keepdims=True),
-            jnp.sum(cot_wide * out, axis=0, keepdims=True),
+            jnp.sum(cot[...].astype(F32) * out, axis=0, keepdims=True),
         ],
         axis=0,
     )
-    normed_grad = back * (1.0 + row(scale))
-    first_mean = jnp.mean(normed_grad, axis=1, keepdims=True)
-    second_mean = jnp.mean(normed_grad * normed, axis=1, keepdims=True)
-    grad_input[...] = (
-        cot_wide + inv_std * (normed_grad - first_mean - normed * second_mean)
-    ).astype(BF16)
-
-
-def finish(items, tokens, scale, gate, qkv_w, out_w, cot):
+
+
+def gather(items, tokens, qkv_w, out_w, cot):
     tok_rows, width = tokens.shape
-    head_size = width // H
     vmem = pl.BlockSpec(memory_space=pltpu.VMEM)
     return pl.pallas_call(
-        functools.partial(finish_kernel, head_size),
-        in_specs=[vmem] * 7,
+        functools.partial(gather_kernel, width // H),
+        in_specs=[vmem] * 5,
         out_specs=[vmem] * 3,
         out_shape=[
-            jax.ShapeDtypeStruct((tok_rows, width), BF16),
-            jax.ShapeDtypeStruct((tok_rows, width), BF16),
+            jax.ShapeDtypeStruct((tok_rows, width), F32),
+            jax.ShapeDtypeStruct((tok_rows, width), F32),
             jax.ShapeDtypeStruct((3, width), F32),
         ],
         scratch_shapes=[pltpu.VMEM((3 * width, tok_rows), BF16)],
         compiler_params=pltpu.CompilerParams(vmem_limit_bytes=FINISH_LIMIT),
+        name="gather",
+    )(items, tokens, qkv_w, out_w, cot)
+
+
+def finish_kernel(branch, mod_grad, tokens, scale, gate, cot, block_output, grad_input):
+    wide, normed, inv_std = normalise(tokens[...])
+    block_output[...] = (wide + row(gate) * branch[...]).astype(BF16)
+    normed_grad = mod_grad[...] * (1.0 + row(scale))
+    first_mean = jnp.mean(normed_grad, axis=1, keepdims=True)
+    second_mean = jnp.mean(normed_grad * normed, axis=1, keepdims=True)
+    grad_input[...] = (
+        cot[...].astype(F32) + inv_std * (normed_grad - first_mean - normed * second_mean)
+    ).astype(BF16)
+
+
+def finish(branch, mod_grad, tokens, scale, gate, cot):
+    vmem = pl.BlockSpec(memory_space=pltpu.VMEM)
+    return pl.pallas_call(
+        finish_kernel,
+        in_specs=[vmem] * 6,
+        out_specs=[vmem] * 2,
+        out_shape=[jax.ShapeDtypeStruct(tokens.shape, BF16)] * 2,
+        compiler_params=pltpu.CompilerParams(vmem_limit_bytes=FINISH_LIMIT),
+        cost_estimate=pl.CostEstimate(
+            flops=30 * tokens.size, transcendentals=0, bytes_accessed=16 * tokens.size
+        ),
         name="finish",
-    )(items, tokens, scale, gate, qkv_w, out_w, cot)
+    )(branch, mod_grad, tokens, scale, gate, cot)
 
 
 def from_partner(shard, axis, stride):
@@ -310,15 +327,15 @@
         back = exchange(made.reshape(seq_count, 4 * head_size, sub_rows))
         returned = back.reshape(H, repeat, 4 * head_size, sub_rows).transpose(0, 2, 1, 3)
         returned = returned.reshape(H, 4 * head_size, tok_rows)
-    block_output, grad_input, sums = finish(
-        returned, tokens, scale_cond, gate_cond, held, out_weight, cotangent
+    branch, mod_grad, sums = gather(returned, tokens, held, out_weight, cotangent)
+    block_output, grad_input = finish(
+        branch, mod_grad, tokens, scale_cond, gate_cond, cotangent
     )
     stride = 1
     while stride < seq_count:
         sums = sums + from_partner(sums, "seq", stride)
         stride *= 2
-    grad_condition = sums / math.sqrt(tok_rows * seq_count)
-    return (block_output, grad_input, grad_condition)
+    return (block_output, grad_input, sums / math.sqrt(tok_rows * seq_count))
 
 
 def solution(mesh):

time: 111 us -> 109 us (0.982)
    ppermute x4, waiting for transfers between devices: 10.1 us -> 9 us  [from_partner(): lax.ppermute(shard, axis, [(i, i ^ stride) for i in range(lax.axis_size(a...]
    pallas_call x2 -> x3, Pallas kernels: 11.3 us -> 11 us  [the longest x1 6.85 us: project(): pl.pallas_call(functools.partial(project_kernel, head_size), in_specs=[hb...]
  transfers between devices with their start and end apart: 4 -> 4, of which waited for: 4 -> 4; matrix products, arithmetic and copies ran while one was open for 0% -> 0% of each run, Pallas kernels for 0% -> 1%
where the time goes in v4:
time: 109 us
  blocking collectives  69.6 us (64%)
  Pallas kernels  25.9 us (24%)
  waiting for transfers between devices  9 us (8%)
  starting transfers between devices  3.29 us (3%)
    all_to_all x2, blocking collectives, exchange(): lax.all_to_all(blocks, 'seq', split_axis=0, concat_axis=0, tiled=True)  69.6 us
    pallas_call x1, Pallas kernels, attend(): pl.pallas_call(functools.partial(attend_kernel, head_size, group, split),...  14.9 us
    ppermute x4, waiting for transfers between devices, from_partner(): lax.ppermute(shard, axis, [(i, i ^ stride) for i in range(lax.axis_size(a...  9 us
    pallas_call x1, Pallas kernels, project(): pl.pallas_call(functools.partial(project_kernel, head_size), in_specs=[hb...  6.85 us
    ppermute x4, starting transfers between devices, from_partner(): lax.ppermute(shard, axis, [(i, i ^ stride) for i in range(lax.axis_size(a...  3.29 us
    pallas_call x1, Pallas kernels, gather(): pl.pallas_call(functools.partial(gather_kernel, width // H), in_specs=[vm...  3.01 us
  transfers between devices with their start and end apart: 4, of which 4 were waited for; matrix products, arithmetic and copies ran while one was open for 0% of the time, Pallas kernels for 1%

profile of v4, /device:TPU:0, one launch (start us, length us, event | category | flops | bytes accessed | tf_op | source)
XLA Modules:
  0.0 109.2 jit_solution(16359634401509373820)
XLA Ops:
  0.6 6.9 %project.1 = bf16[16,288,128]{2,1,0:T(8,128)(2,1)} custom-call(bf16[128,1152]{1,0:T(8,128)(2,1)} %tokens.3, f32[1152]{0:T(1024)} %refs_1_.1, f32[1152]{0:T(1024)} %scale.1, f32[1152]{0:T(1024)} %gate.1, bf16[128,1152]{1,0:T(8,128)(2,1)} %cot.3, bf16[1152,1152]{1,0:T(8,128)(2,1)} %out_w.1, bf16[1152,3456]{1,0:T(8,128)(2,1)} %weight.1), custom_call_target="tpu_custom_call" | custom-call | tf_op jit(solution)/shard_map/project/pallas_call | solution.py:88
  7.5 36.9 %all_to_all.10.items = bf16[16,288,128]{2,1,0:T(8,128)(2,1)S(1)} all-to-all(bf16[16,288,128]{2,1,0:T(8,128)(2,1)} %project.1), channel_id=1, replica_groups=mesh['groups'=2,'seq'=16] {'seq'}, dimensions={0} | all-to-all | bytes 2359296 | tf_op jit(solution)/shard_map/all_to_all | solution.py:299
  44.4 14.9 %attend.1 = (bf16[1152,3456]{1,0:T(8,128)(2,1)S(1)}, bf16[16,288,128]{2,1,0:T(8,128)(2,1)S(1)}) custom-call(bf16[16,288,128]{2,1,0:T(8,128)(2,1)S(1)} %all_to_all.10.items, bf16[1152,3456]{1,0:T(8,128)(2,1)} %weight.1), custom_call_target="tpu_custom_call" | custom-call | tf_op jit(solution)/shard_map/attend/pallas_call | solution.py:204
  59.3 0.0 copy-start.1
  59.3 0.0 copy-start.2
  59.3 32.7 %all_to_all.11.items = bf16[16,288,128]{2,1,0:T(8,128)(2,1)S(1)} all-to-all(bf16[16,288,128]{2,1,0:T(8,128)(2,1)S(1)} %get-tuple-element.10), channel_id=1, replica_groups=mesh['groups'=2,'seq'=16] {'seq'}, dimensions={0} | all-to-all | bytes 2359296 | tf_op jit(solution)/shard_map/all_to_all | solution.py:299
  92.1 0.0 copy-done
  92.1 0.0 copy-done.1
  92.1 0.0 copy-done.2
  92.1 0.0 copy-start.3
  92.1 0.0 copy-start.4
  92.1 3.0 %gather.1 = (f32[128,1152]{1,0:T(8,128)S(1)}, f32[128,1152]{1,0:T(8,128)S(1)}, f32[3,1152]{1,0:T(4,128)S(1)}) custom-call(bf16[16,288,128]{2,1,0:T(8,128)(2,1)S(1)} %all_to_all.11.items, bf16[128,1152]{1,0:T(8,128)(2,1)S(1)} %copy-done.1, bf16[1152,3456]{1,0:T(8,128)(2,1)S(1)} %get-tuple-element.11.qkv_w, bf16[1152,1152]{1,0:T(8,128)(2,1)S(1)} %copy-done, ...), custom_call_target="tpu_custom_call" | custom-call | tf_op jit(solution)/shard_map/gather/pallas_call | solution.py:253
  95.1 0.4 collective-permute-start
  95.5 0.9 collective-permute-done
  96.4 0.7 collective-permute-start.1
  97.1 3.0 %collective-permute-done.1 = f32[3,1152]{1,0:T(4,128)S(1)} collective-permute-done((f32[3,1152]{1,0:T(4,128)S(1)}, f32[3,1152]{1,0:T(4,128)S(1)}, u32[]{:S(2)}, u32[]{:S(2)}) %collective-permute-start.1) | collective-permute-done | bytes 13856 | tf_op jit(solution)/shard_map/ppermute | solution.py:295
  100.1 0.9 collective-permute-start.2
  101.0 2.9 %collective-permute-done.2 = f32[3,1152]{1,0:T(4,128)S(1)} collective-permute-done((f32[3,1152]{1,0:T(4,128)S(1)}, f32[3,1152]{1,0:T(4,128)S(1)}, u32[]{:S(2)}, u32[]{:S(2)}) %collective-permute-start.2) | collective-permute-done | bytes 13856 | tf_op jit(solution)/shard_map/ppermute | solution.py:295
  103.9 1.3 %collective-permute-start.3 = (f32[3,1152]{1,0:T(4,128)S(1)}, f32[3,1152]{1,0:T(4,128)S(1)}, u32[]{:S(2)}, u32[]{:S(2)}) collective-permute-start(f32[3,1152]{1,0:T(4,128)S(1)} %add.14), channel_id=1, source_target_pairs={{0,8},{1,9},{2,10},{3,11},{4,12},{5,13},{6,14},{7,15},{8,0},{9,1},... | collective-permute-start | bytes 41480 | tf_op jit(solution)/shard_map/ppermute | solution.py:295
  105.2 0.0 copy-done.3
  105.2 0.0 copy-done.4
  105.2 1.1 %finish.1 = (bf16[128,1152]{1,0:T(8,128)(2,1)}, bf16[128,1152]{1,0:T(8,128)(2,1)}) custom-call(f32[128,1152]{1,0:T(8,128)S(1)} %get-tuple-element.12.branch, f32[128,1152]{1,0:T(8,128)S(1)} %get-tuple-element.13.mod_grad, bf16[128,1152]{1,0:T(8,128)(2,1)S(1)} %copy-done.1, f32[1152]{0:T(1024)S(1)} %copy-done.3, f32[1152]{0:T(1024)S(1)} %copy-done.4, ...), custom_call_target="tpu_custom_call" | custom-call | flops 4423680 | bytes 2359296 | tf_op jit(solution)/shard_map/finish/pallas_call | solution.py:281
  106.3 2.2 %collective-permute-done.3 = f32[3,1152]{1,0:T(4,128)S(1)} collective-permute-done((f32[3,1152]{1,0:T(4,128)S(1)}, f32[3,1152]{1,0:T(4,128)S(1)}, u32[]{:S(2)}, u32[]{:S(2)}) %collective-permute-start.3) | collective-permute-done | bytes 13856 | tf_op jit(solution)/shard_map/ppermute | solution.py:295
  108.6 0.6 add_multiply_fusion
  (4 shorter events, 0.0 us)
Async XLA Ops:
  44.4 47.7 %copy-start = (bf16[1152,1152]{1,0:T(8,128)(2,1)S(1)}, bf16[1152,1152]{1,0:T(8,128)(2,1)}, u32[]{:S(2)}) copy-start(bf16[1152,1152]{1,0:T(8,128)(2,1)} %out_w.1) | copy-start | bytes 7962628
  59.3 32.7 %copy-start.1 = (bf16[128,1152]{1,0:T(8,128)(2,1)S(1)}, bf16[128,1152]{1,0:T(8,128)(2,1)}, u32[]{:S(2)}) copy-start(bf16[128,1152]{1,0:T(8,128)(2,1)} %tokens.3) | copy-start | bytes 884740
  59.3 32.7 %copy-start.2 = (bf16[128,1152]{1,0:T(8,128)(2,1)S(1)}, bf16[128,1152]{1,0:T(8,128)(2,1)}, u32[]{:S(2)}) copy-start(bf16[128,1152]{1,0:T(8,128)(2,1)} %cot.3) | copy-start | bytes 884740
  92.1 13.1 %copy-start.3 = (f32[1152]{0:T(1024)S(1)}, f32[1152]{0:T(1024)}, u32[]{:S(2)}) copy-start(f32[1152]{0:T(1024)} %scale.1) | copy-start | bytes 13828
  92.1 13.1 %copy-start.4 = (f32[1152]{0:T(1024)S(1)}, f32[1152]{0:T(1024)}, u32[]{:S(2)}) copy-start(f32[1152]{0:T(1024)} %gate.1) | copy-start | bytes 13828
  95.1 1.3 %collective-permute-start = (f32[3,1152]{1,0:T(4,128)S(1)}, f32[3,1152]{1,0:T(4,128)S(1)}, u32[]{:S(2)}, u32[]{:S(2)}) collective-permute-start(f32[3,1152]{1,0:T(4,128)S(1)} %get-tuple-element.16), channel_id=1, source_target_pairs={{0,1},{1,0},{2,3},{3,2},{4,5},{5,4},{6,7},{7,6},{8,9},{9,8},{10,11... | collective-permute-start | bytes 41480 | tf_op jit(solution)/shard_map/ppermute | solution.py:295
  96.4 3.8 %collective-permute-start.1 = (f32[3,1152]{1,0:T(4,128)S(1)}, f32[3,1152]{1,0:T(4,128)S(1)}, u32[]{:S(2)}, u32[]{:S(2)}) collective-permute-start(f32[3,1152]{1,0:T(4,128)S(1)} %add.12), channel_id=1, source_target_pairs={{0,2},{1,3},{2,0},{3,1},{4,6},{5,7},{6,4},{7,5},{8,10},{9,11},{10,... | collective-permute-start | bytes 41480 | tf_op jit(solution)/shard_map/ppermute | solution.py:295
  100.1 3.8 %collective-permute-start.2 = (f32[3,1152]{1,0:T(4,128)S(1)}, f32[3,1152]{1,0:T(4,128)S(1)}, u32[]{:S(2)}, u32[]{:S(2)}) collective-permute-start(f32[3,1152]{1,0:T(4,128)S(1)} %add.13), channel_id=1, source_target_pairs={{0,4},{1,5},{2,6},{3,7},{4,0},{5,1},{6,2},{7,3},{8,12},{9,13},{10,... | collective-permute-start | bytes 41480 | tf_op jit(solution)/shard_map/ppermute | solution.py:295
  103.9 4.7 %collective-permute-start.3 = (f32[3,1152]{1,0:T(4,128)S(1)}, f32[3,1152]{1,0:T(4,128)S(1)}, u32[]{:S(2)}, u32[]{:S(2)}) collective-permute-start(f32[3,1152]{1,0:T(4,128)S(1)} %add.14), channel_id=1, source_target_pairs={{0,8},{1,9},{2,10},{3,11},{4,12},{5,13},{6,14},{7,15},{8,0},{9,1},... | collective-permute-start | bytes 41480 | tf_op jit(solution)/shard_map/ppermute | solution.py:295

commit v5 on v4

--- a/solution.py
+++ b/solution.py
@@ -333,8 +333,13 @@
     )
     stride = 1
     while stride < seq_count:
-        sums = sums + from_partner(sums, "seq", stride)
-        stride *= 2
+        if stride == 2 and seq_count >= 8:
+            first, second, third = (from_partner(sums, "seq", k * stride) for k in (1, 2, 3))
+            sums = (sums + first) + (second + third)
+            stride *= 4
+        else:
+            sums = sums + from_partner(sums, "seq", stride)
+            stride *= 2
     return (block_output, grad_input, sums / math.sqrt(tok_rows * seq_count))
 
 

time: 109 us -> 108 us (level)
  waiting for transfers between devices: 9 us -> 6.27 us
  starting transfers between devices: 3.29 us -> 4.53 us
    ppermute x4 -> x5, waiting for transfers between devices: 9 us -> 6.27 us  [from_partner(): lax.ppermute(shard, axis, [(i, i ^ stride) for i in range(lax.axis_size(a...]
    ppermute x4 -> x5, starting transfers between devices: 3.29 us -> 4.53 us  [from_partner(): lax.ppermute(shard, axis, [(i, i ^ stride) for i in range(lax.axis_size(a...]
  transfers between devices with their start and end apart: 4 -> 5, of which waited for: 4 -> 4; matrix products, arithmetic and copies ran while one was open for 0% -> 0% of each run, Pallas kernels for 1% -> 1%
where the time goes in v5:
time: 108 us
  blocking collectives  69.6 us (64%)
  Pallas kernels  26 us (24%)
  waiting for transfers between devices  6.27 us (6%)
  starting transfers between devices  4.53 us (4%)
    all_to_all x2, blocking collectives, exchange(): lax.all_to_all(blocks, 'seq', split_axis=0, concat_axis=0, tiled=True)  69.6 us
    pallas_call x1, Pallas kernels, attend(): pl.pallas_call(functools.partial(attend_kernel, head_size, group, split),...  14.9 us
    pallas_call x1, Pallas kernels, project(): pl.pallas_call(functools.partial(project_kernel, head_size), in_specs=[hb...  6.86 us
    ppermute x5, waiting for transfers between devices, from_partner(): lax.ppermute(shard, axis, [(i, i ^ stride) for i in range(lax.axis_size(a...  6.27 us
    ppermute x5, starting transfers between devices, from_partner(): lax.ppermute(shard, axis, [(i, i ^ stride) for i in range(lax.axis_size(a...  4.53 us
    pallas_call x1, Pallas kernels, gather(): pl.pallas_call(functools.partial(gather_kernel, width // H), in_specs=[vm...  3.01 us
  transfers between devices with their start and end apart: 5, of which 4 were waited for; matrix products, arithmetic and copies ran while one was open for 0% of the time, Pallas kernels for 1%

profile of v5, /device:TPU:0, one launch (start us, length us, event | category | flops | bytes accessed | tf_op | source)
XLA Modules:
  0.0 107.7 jit_solution(10730766959216812676)
XLA Ops:
  0.6 6.9 %project.1 = bf16[16,288,128]{2,1,0:T(8,128)(2,1)} custom-call(bf16[128,1152]{1,0:T(8,128)(2,1)} %tokens.3, f32[1152]{0:T(1024)} %refs_1_.1, f32[1152]{0:T(1024)} %scale.1, f32[1152]{0:T(1024)} %gate.1, bf16[128,1152]{1,0:T(8,128)(2,1)} %cot.3, bf16[1152,1152]{1,0:T(8,128)(2,1)} %out_w.1, bf16[1152,3456]{1,0:T(8,128)(2,1)} %weight.1), custom_call_target="tpu_custom_call" | custom-call | tf_op jit(solution)/shard_map/project/pallas_call | solution.py:88
  7.5 36.9 %all_to_all.10.items = bf16[16,288,128]{2,1,0:T(8,128)(2,1)S(1)} all-to-all(bf16[16,288,128]{2,1,0:T(8,128)(2,1)} %project.1), channel_id=1, replica_groups=mesh['groups'=2,'seq'=16] {'seq'}, dimensions={0} | all-to-all | bytes 2359296 | tf_op jit(solution)/shard_map/all_to_all | solution.py:299
  44.4 14.9 %attend.1 = (bf16[1152,3456]{1,0:T(8,128)(2,1)S(1)}, bf16[16,288,128]{2,1,0:T(8,128)(2,1)S(1)}) custom-call(bf16[16,288,128]{2,1,0:T(8,128)(2,1)S(1)} %all_to_all.10.items, bf16[1152,3456]{1,0:T(8,128)(2,1)} %weight.1), custom_call_target="tpu_custom_call" | custom-call | tf_op jit(solution)/shard_map/attend/pallas_call | solution.py:204
  59.3 0.0 copy-start.1
  59.3 0.0 copy-start.2
  59.4 32.7 %all_to_all.11.items = bf16[16,288,128]{2,1,0:T(8,128)(2,1)S(1)} all-to-all(bf16[16,288,128]{2,1,0:T(8,128)(2,1)S(1)} %get-tuple-element.10), channel_id=1, replica_groups=mesh['groups'=2,'seq'=16] {'seq'}, dimensions={0} | all-to-all | bytes 2359296 | tf_op jit(solution)/shard_map/all_to_all | solution.py:299
  92.1 0.0 copy-done
  92.1 0.0 copy-done.1
  92.1 0.0 copy-done.2
  92.1 0.0 copy-start.3
  92.1 0.0 copy-start.4
  92.1 3.0 %gather.1 = (f32[128,1152]{1,0:T(8,128)S(1)}, f32[128,1152]{1,0:T(8,128)S(1)}, f32[3,1152]{1,0:T(4,128)S(1)}) custom-call(bf16[16,288,128]{2,1,0:T(8,128)(2,1)S(1)} %all_to_all.11.items, bf16[128,1152]{1,0:T(8,128)(2,1)S(1)} %copy-done.1, bf16[1152,3456]{1,0:T(8,128)(2,1)S(1)} %get-tuple-element.11.qkv_w, bf16[1152,1152]{1,0:T(8,128)(2,1)S(1)} %copy-done, ...), custom_call_target="tpu_custom_call" | custom-call | tf_op jit(solution)/shard_map/gather/pallas_call | solution.py:253
  95.1 0.4 collective-permute-start
  95.5 0.9 collective-permute-done
  96.4 1.0 collective-permute-start.3
  97.3 1.2 %collective-permute-start.2 = (f32[3,1152]{1,0:T(4,128)S(1)}, f32[3,1152]{1,0:T(4,128)S(1)}, u32[]{:S(2)}, u32[]{:S(2)}) collective-permute-start(f32[3,1152]{1,0:T(4,128)S(1)} %add.15), channel_id=1, source_target_pairs={{0,4},{1,5},{2,6},{3,7},{4,0},{5,1},{6,2},{7,3},{8,12},{9,13},{10,... | collective-permute-start | bytes 41480 | tf_op jit(solution)/shard_map/ppermute | solution.py:295
  98.6 1.3 %collective-permute-start.1 = (f32[3,1152]{1,0:T(4,128)S(1)}, f32[3,1152]{1,0:T(4,128)S(1)}, u32[]{:S(2)}, u32[]{:S(2)}) collective-permute-start(f32[3,1152]{1,0:T(4,128)S(1)} %add.15), channel_id=1, source_target_pairs={{0,2},{1,3},{2,0},{3,1},{4,6},{5,7},{6,4},{7,5},{8,10},{9,11},{10,... | collective-permute-start | bytes 41480 | tf_op jit(solution)/shard_map/ppermute | solution.py:295
  99.9 1.3 %collective-permute-done.3 = f32[3,1152]{1,0:T(4,128)S(1)} collective-permute-done((f32[3,1152]{1,0:T(4,128)S(1)}, f32[3,1152]{1,0:T(4,128)S(1)}, u32[]{:S(2)}, u32[]{:S(2)}) %collective-permute-start.3) | collective-permute-done | bytes 13856 | tf_op jit(solution)/shard_map/ppermute | solution.py:295
  101.1 0.0 collective-permute-done.2
  101.1 1.2 %collective-permute-done.1 = f32[3,1152]{1,0:T(4,128)S(1)} collective-permute-done((f32[3,1152]{1,0:T(4,128)S(1)}, f32[3,1152]{1,0:T(4,128)S(1)}, u32[]{:S(2)}, u32[]{:S(2)}) %collective-permute-start.1) | collective-permute-done | bytes 13856 | tf_op jit(solution)/shard_map/ppermute | solution.py:295
  102.3 0.7 collective-permute-start.4
  103.0 1.1 %finish.1 = (bf16[128,1152]{1,0:T(8,128)(2,1)}, bf16[128,1152]{1,0:T(8,128)(2,1)}) custom-call(f32[128,1152]{1,0:T(8,128)S(1)} %get-tuple-element.12.branch, f32[128,1152]{1,0:T(8,128)S(1)} %get-tuple-element.13.mod_grad, bf16[128,1152]{1,0:T(8,128)(2,1)S(1)} %copy-done.1, f32[1152]{0:T(1024)S(1)} %copy-done.3, f32[1152]{0:T(1024)S(1)} %copy-done.4, ...), custom_call_target="tpu_custom_call" | custom-call | flops 4423680 | bytes 2359296 | tf_op jit(solution)/shard_map/finish/pallas_call | solution.py:281
  104.2 2.9 %collective-permute-done.4 = f32[3,1152]{1,0:T(4,128)S(1)} collective-permute-done((f32[3,1152]{1,0:T(4,128)S(1)}, f32[3,1152]{1,0:T(4,128)S(1)}, u32[]{:S(2)}, u32[]{:S(2)}) %collective-permute-start.4) | collective-permute-done | bytes 13856 | tf_op jit(solution)/shard_map/ppermute | solution.py:295
  107.1 0.6 add_multiply_fusion
  (5 shorter events, 0.0 us)
Async XLA Ops:
  44.4 47.7 %copy-start = (bf16[1152,1152]{1,0:T(8,128)(2,1)S(1)}, bf16[1152,1152]{1,0:T(8,128)(2,1)}, u32[]{:S(2)}) copy-start(bf16[1152,1152]{1,0:T(8,128)(2,1)} %out_w.1) | copy-start | bytes 7962628
  59.3 32.7 %copy-start.1 = (bf16[128,1152]{1,0:T(8,128)(2,1)S(1)}, bf16[128,1152]{1,0:T(8,128)(2,1)}, u32[]{:S(2)}) copy-start(bf16[128,1152]{1,0:T(8,128)(2,1)} %tokens.3) | copy-start | bytes 884740
  59.3 32.7 %copy-start.2 = (bf16[128,1152]{1,0:T(8,128)(2,1)S(1)}, bf16[128,1152]{1,0:T(8,128)(2,1)}, u32[]{:S(2)}) copy-start(bf16[128,1152]{1,0:T(8,128)(2,1)} %cot.3) | copy-start | bytes 884740
  92.1 10.9 %copy-start.3 = (f32[1152]{0:T(1024)S(1)}, f32[1152]{0:T(1024)}, u32[]{:S(2)}) copy-start(f32[1152]{0:T(1024)} %scale.1) | copy-start | bytes 13828
  92.1 10.9 %copy-start.4 = (f32[1152]{0:T(1024)S(1)}, f32[1152]{0:T(1024)}, u32[]{:S(2)}) copy-start(f32[1152]{0:T(1024)} %gate.1) | copy-start | bytes 13828
  95.1 1.3 %collective-permute-start = (f32[3,1152]{1,0:T(4,128)S(1)}, f32[3,1152]{1,0:T(4,128)S(1)}, u32[]{:S(2)}, u32[]{:S(2)}) collective-permute-start(f32[3,1152]{1,0:T(4,128)S(1)} %get-tuple-element.16), channel_id=1, source_target_pairs={{0,1},{1,0},{2,3},{3,2},{4,5},{5,4},{6,7},{7,6},{8,9},{9,8},{10,11... | collective-permute-start | bytes 41480 | tf_op jit(solution)/shard_map/ppermute | solution.py:295
  96.4 4.8 %collective-permute-start.3 = (f32[3,1152]{1,0:T(4,128)S(1)}, f32[3,1152]{1,0:T(4,128)S(1)}, u32[]{:S(2)}, u32[]{:S(2)}) collective-permute-start(f32[3,1152]{1,0:T(4,128)S(1)} %add.15), channel_id=1, source_target_pairs={{0,6},{1,7},{2,4},{3,5},{4,2},{5,3},{6,0},{7,1},{8,14},{9,15},{10,... | collective-permute-start | bytes 41480 | tf_op jit(solution)/shard_map/ppermute | solution.py:295
  97.3 3.8 %collective-permute-start.2 = (f32[3,1152]{1,0:T(4,128)S(1)}, f32[3,1152]{1,0:T(4,128)S(1)}, u32[]{:S(2)}, u32[]{:S(2)}) collective-permute-start(f32[3,1152]{1,0:T(4,128)S(1)} %add.15), channel_id=1, source_target_pairs={{0,4},{1,5},{2,6},{3,7},{4,0},{5,1},{6,2},{7,3},{8,12},{9,13},{10,... | collective-permute-start | bytes 41480 | tf_op jit(solution)/shard_map/ppermute | solution.py:295
  98.6 3.8 %collective-permute-start.1 = (f32[3,1152]{1,0:T(4,128)S(1)}, f32[3,1152]{1,0:T(4,128)S(1)}, u32[]{:S(2)}, u32[]{:S(2)}) collective-permute-start(f32[3,1152]{1,0:T(4,128)S(1)} %add.15), channel_id=1, source_target_pairs={{0,2},{1,3},{2,0},{3,1},{4,6},{5,7},{6,4},{7,5},{8,10},{9,11},{10,... | collective-permute-start | bytes 41480 | tf_op jit(solution)/shard_map/ppermute | solution.py:295
  102.3 4.7 %collective-permute-start.4 = (f32[3,1152]{1,0:T(4,128)S(1)}, f32[3,1152]{1,0:T(4,128)S(1)}, u32[]{:S(2)}, u32[]{:S(2)}) collective-permute-start(f32[3,1152]{1,0:T(4,128)S(1)} %add_add_fusion), channel_id=1, source_target_pairs={{0,8},{1,9},{2,10},{3,11},{4,12},{5,13},{6,14},{7,15},{8,0},{9,1},... | collective-permute-start | bytes 41480 | tf_op jit(solution)/shard_map/ppermute | solution.py:295

commit v6 on v5

--- a/solution.py
+++ b/solution.py
@@ -333,7 +333,7 @@
     )
     stride = 1
     while stride < seq_count:
-        if stride == 2 and seq_count >= 8:
+        if 4 * stride <= seq_count:
             first, second, third = (from_partner(sums, "seq", k * stride) for k in (1, 2, 3))
             sums = (sums + first) + (second + third)
             stride *= 4

time: 108 us -> 107 us (level)
  waiting for transfers between devices: 6.27 us -> 3.2 us
  starting transfers between devices: 4.53 us -> 6.46 us
    ppermute x5 -> x6, waiting for transfers between devices: 6.27 us -> 3.2 us  [from_partner(): lax.ppermute(shard, axis, [(i, i ^ stride) for i in range(lax.axis_size(a...]
    ppermute x5 -> x6, starting transfers between devices: 4.53 us -> 6.46 us  [from_partner(): lax.ppermute(shard, axis, [(i, i ^ stride) for i in range(lax.axis_size(a...]
  transfers between devices with their start and end apart: 5 -> 6, of which waited for: 4 -> 4; matrix products, arithmetic and copies ran while one was open for 0% -> 0% of each run, Pallas kernels for 1% -> 1%
where the time goes in v6:
time: 107 us
  blocking collectives  69.6 us (65%)
  Pallas kernels  25.9 us (24%)
  starting transfers between devices  6.46 us (6%)
  waiting for transfers between devices  3.2 us (3%)
    all_to_all x2, blocking collectives, exchange(): lax.all_to_all(blocks, 'seq', split_axis=0, concat_axis=0, tiled=True)  69.6 us
    pallas_call x1, Pallas kernels, attend(): pl.pallas_call(functools.partial(attend_kernel, head_size, group, split),...  14.9 us
    pallas_call x1, Pallas kernels, project(): pl.pallas_call(functools.partial(project_kernel, head_size), in_specs=[hb...  6.88 us
    ppermute x6, starting transfers between devices, from_partner(): lax.ppermute(shard, axis, [(i, i ^ stride) for i in range(lax.axis_size(a...  6.46 us
    ppermute x6, waiting for transfers between devices, from_partner(): lax.ppermute(shard, axis, [(i, i ^ stride) for i in range(lax.axis_size(a...  3.2 us
    pallas_call x1, Pallas kernels, gather(): pl.pallas_call(functools.partial(gather_kernel, width // H), in_specs=[vm...  3.01 us
  transfers between devices with their start and end apart: 6, of which 4 were waited for; matrix products, arithmetic and copies ran while one was open for 0% of the time, Pallas kernels for 1%

profile of v6, /device:TPU:0, one launch (start us, length us, event | category | flops | bytes accessed | tf_op | source)
XLA Modules:
  0.0 106.6 jit_solution(12558773012849697448)
XLA Ops:
  0.6 6.9 %project.1 = bf16[16,288,128]{2,1,0:T(8,128)(2,1)} custom-call(bf16[128,1152]{1,0:T(8,128)(2,1)} %tokens.3, f32[1152]{0:T(1024)} %refs_1_.1, f32[1152]{0:T(1024)} %scale.1, f32[1152]{0:T(1024)} %gate.1, bf16[128,1152]{1,0:T(8,128)(2,1)} %cot.3, bf16[1152,1152]{1,0:T(8,128)(2,1)} %out_w.1, bf16[1152,3456]{1,0:T(8,128)(2,1)} %weight.1), custom_call_target="tpu_custom_call" | custom-call | tf_op jit(solution)/shard_map/project/pallas_call | solution.py:88
  7.5 36.9 %all_to_all.10.items = bf16[16,288,128]{2,1,0:T(8,128)(2,1)S(1)} all-to-all(bf16[16,288,128]{2,1,0:T(8,128)(2,1)} %project.1), channel_id=1, replica_groups=mesh['groups'=2,'seq'=16] {'seq'}, dimensions={0} | all-to-all | bytes 2359296 | tf_op jit(solution)/shard_map/all_to_all | solution.py:299
  44.4 14.9 %attend.1 = (bf16[1152,3456]{1,0:T(8,128)(2,1)S(1)}, bf16[16,288,128]{2,1,0:T(8,128)(2,1)S(1)}) custom-call(bf16[16,288,128]{2,1,0:T(8,128)(2,1)S(1)} %all_to_all.10.items, bf16[1152,3456]{1,0:T(8,128)(2,1)} %weight.1), custom_call_target="tpu_custom_call" | custom-call | tf_op jit(solution)/shard_map/attend/pallas_call | solution.py:204
  59.3 0.0 copy-start.1
  59.3 0.0 copy-start.2
  59.4 32.7 %all_to_all.11.items = bf16[16,288,128]{2,1,0:T(8,128)(2,1)S(1)} all-to-all(bf16[16,288,128]{2,1,0:T(8,128)(2,1)S(1)} %get-tuple-element.10), channel_id=1, replica_groups=mesh['groups'=2,'seq'=16] {'seq'}, dimensions={0} | all-to-all | bytes 2359296 | tf_op jit(solution)/shard_map/all_to_all | solution.py:299
  92.1 0.0 copy-done
  92.1 0.0 copy-start.3
  92.1 0.0 copy-start.4
  92.1 3.0 %gather.1 = (f32[128,1152]{1,0:T(8,128)S(1)}, f32[128,1152]{1,0:T(8,128)S(1)}, f32[3,1152]{1,0:T(4,128)S(1)}) custom-call(bf16[16,288,128]{2,1,0:T(8,128)(2,1)S(1)} %all_to_all.11.items, bf16[128,1152]{1,0:T(8,128)(2,1)S(1)} %copy-done.1, bf16[1152,3456]{1,0:T(8,128)(2,1)S(1)} %get-tuple-element.11.qkv_w, bf16[1152,1152]{1,0:T(8,128)(2,1)S(1)} %copy-done, ...), custom_call_target="tpu_custom_call" | custom-call | tf_op jit(solution)/shard_map/gather/pallas_call | solution.py:253
  95.1 0.6 collective-permute-start.2
  95.8 1.4 %collective-permute-start.1 = (f32[3,1152]{1,0:T(4,128)S(1)}, f32[3,1152]{1,0:T(4,128)S(1)}, u32[]{:S(2)}, u32[]{:S(2)}) collective-permute-start(f32[3,1152]{1,0:T(4,128)S(1)} %get-tuple-element.16), channel_id=1, source_target_pairs={{0,2},{1,3},{2,0},{3,1},{4,6},{5,7},{6,4},{7,5},{8,10},{9,11},{10,... | collective-permute-start | bytes 41480 | tf_op jit(solution)/shard_map/ppermute | solution.py:295
  97.1 0.0 collective-permute-start
  97.1 1.2 %collective-permute-done.2 = f32[3,1152]{1,0:T(4,128)S(1)} collective-permute-done((f32[3,1152]{1,0:T(4,128)S(1)}, f32[3,1152]{1,0:T(4,128)S(1)}, u32[]{:S(2)}, u32[]{:S(2)}) %collective-permute-start.2) | collective-permute-done | bytes 13856 | tf_op jit(solution)/shard_map/ppermute | solution.py:295
  98.4 1.2 %collective-permute-done.1 = f32[3,1152]{1,0:T(4,128)S(1)} collective-permute-done((f32[3,1152]{1,0:T(4,128)S(1)}, f32[3,1152]{1,0:T(4,128)S(1)}, u32[]{:S(2)}, u32[]{:S(2)}) %collective-permute-start.1) | collective-permute-done | bytes 13856 | tf_op jit(solution)/shard_map/ppermute | solution.py:295
  99.5 0.0 collective-permute-done
  99.5 1.7 %collective-permute-start.5 = (f32[3,1152]{1,0:T(4,128)S(1)}, f32[3,1152]{1,0:T(4,128)S(1)}, u32[]{:S(2)}, u32[]{:S(2)}) collective-permute-start(f32[3,1152]{1,0:T(4,128)S(1)} %add_add_fusion), channel_id=1, source_target_pairs={{0,12},{1,13},{2,14},{3,15},{4,8},{5,9},{6,10},{7,11},{8,4},{9,5},... | collective-permute-start | bytes 41480 | tf_op jit(solution)/shard_map/ppermute | solution.py:295
  101.3 0.5 collective-permute-start.4
  101.8 2.2 %collective-permute-start.3 = (f32[3,1152]{1,0:T(4,128)S(1)}, f32[3,1152]{1,0:T(4,128)S(1)}, u32[]{:S(2)}, u32[]{:S(2)}) collective-permute-start(f32[3,1152]{1,0:T(4,128)S(1)} %add_add_fusion), channel_id=1, source_target_pairs={{0,4},{1,5},{2,6},{3,7},{4,0},{5,1},{6,2},{7,3},{8,12},{9,13},{10,... | collective-permute-start | bytes 41480 | tf_op jit(solution)/shard_map/ppermute | solution.py:295
  104.0 1.1 %finish.1 = (bf16[128,1152]{1,0:T(8,128)(2,1)}, bf16[128,1152]{1,0:T(8,128)(2,1)}) custom-call(f32[128,1152]{1,0:T(8,128)S(1)} %get-tuple-element.12.branch, f32[128,1152]{1,0:T(8,128)S(1)} %get-tuple-element.13.mod_grad, bf16[128,1152]{1,0:T(8,128)(2,1)S(1)} %copy-done.1, f32[1152]{0:T(1024)S(1)} %copy-done.3, f32[1152]{0:T(1024)S(1)} %copy-done.4, ...), custom_call_target="tpu_custom_call" | custom-call | flops 4423680 | bytes 2359296 | tf_op jit(solution)/shard_map/finish/pallas_call | solution.py:281
  105.2 0.1 collective-permute-done.5
  105.3 0.7 collective-permute-done.4
  106.0 0.0 collective-permute-done.3
  106.0 0.6 add_multiply_fusion
  (6 shorter events, 0.0 us)
Async XLA Ops:
  44.4 47.7 %copy-start = (bf16[1152,1152]{1,0:T(8,128)(2,1)S(1)}, bf16[1152,1152]{1,0:T(8,128)(2,1)}, u32[]{:S(2)}) copy-start(bf16[1152,1152]{1,0:T(8,128)(2,1)} %out_w.1) | copy-start | bytes 7962628
  59.3 32.8 %copy-start.1 = (bf16[128,1152]{1,0:T(8,128)(2,1)S(1)}, bf16[128,1152]{1,0:T(8,128)(2,1)}, u32[]{:S(2)}) copy-start(bf16[128,1152]{1,0:T(8,128)(2,1)} %tokens.3) | copy-start | bytes 884740
  59.3 32.7 %copy-start.2 = (bf16[128,1152]{1,0:T(8,128)(2,1)S(1)}, bf16[128,1152]{1,0:T(8,128)(2,1)}, u32[]{:S(2)}) copy-start(bf16[128,1152]{1,0:T(8,128)(2,1)} %cot.3) | copy-start | bytes 884740
  92.1 11.9 %copy-start.3 = (f32[1152]{0:T(1024)S(1)}, f32[1152]{0:T(1024)}, u32[]{:S(2)}) copy-start(f32[1152]{0:T(1024)} %scale.1) | copy-start | bytes 13828
  92.1 11.9 %copy-start.4 = (f32[1152]{0:T(1024)S(1)}, f32[1152]{0:T(1024)}, u32[]{:S(2)}) copy-start(f32[1152]{0:T(1024)} %gate.1) | copy-start | bytes 13828
  95.1 3.3 %collective-permute-start.2 = (f32[3,1152]{1,0:T(4,128)S(1)}, f32[3,1152]{1,0:T(4,128)S(1)}, u32[]{:S(2)}, u32[]{:S(2)}) collective-permute-start(f32[3,1152]{1,0:T(4,128)S(1)} %get-tuple-element.16), channel_id=1, source_target_pairs={{0,3},{1,2},{2,1},{3,0},{4,7},{5,6},{6,5},{7,4},{8,11},{9,10},{10,... | collective-permute-start | bytes 41480 | tf_op jit(solution)/shard_map/ppermute | solution.py:295
  95.8 3.8 %collective-permute-start.1 = (f32[3,1152]{1,0:T(4,128)S(1)}, f32[3,1152]{1,0:T(4,128)S(1)}, u32[]{:S(2)}, u32[]{:S(2)}) collective-permute-start(f32[3,1152]{1,0:T(4,128)S(1)} %get-tuple-element.16), channel_id=1, source_target_pairs={{0,2},{1,3},{2,0},{3,1},{4,6},{5,7},{6,4},{7,5},{8,10},{9,11},{10,... | collective-permute-start | bytes 41480 | tf_op jit(solution)/shard_map/ppermute | solution.py:295
  97.1 2.4 %collective-permute-start = (f32[3,1152]{1,0:T(4,128)S(1)}, f32[3,1152]{1,0:T(4,128)S(1)}, u32[]{:S(2)}, u32[]{:S(2)}) collective-permute-start(f32[3,1152]{1,0:T(4,128)S(1)} %get-tuple-element.16), channel_id=1, source_target_pairs={{0,1},{1,0},{2,3},{3,2},{4,5},{5,4},{6,7},{7,6},{8,9},{9,8},{10,11... | collective-permute-start | bytes 41480 | tf_op jit(solution)/shard_map/ppermute | solution.py:295
  99.5 5.7 %collective-permute-start.5 = (f32[3,1152]{1,0:T(4,128)S(1)}, f32[3,1152]{1,0:T(4,128)S(1)}, u32[]{:S(2)}, u32[]{:S(2)}) collective-permute-start(f32[3,1152]{1,0:T(4,128)S(1)} %add_add_fusion), channel_id=1, source_target_pairs={{0,12},{1,13},{2,14},{3,15},{4,8},{5,9},{6,10},{7,11},{8,4},{9,5},... | collective-permute-start | bytes 41480 | tf_op jit(solution)/shard_map/ppermute | solution.py:295
  101.3 4.7 %collective-permute-start.4 = (f32[3,1152]{1,0:T(4,128)S(1)}, f32[3,1152]{1,0:T(4,128)S(1)}, u32[]{:S(2)}, u32[]{:S(2)}) collective-permute-start(f32[3,1152]{1,0:T(4,128)S(1)} %add_add_fusion), channel_id=1, source_target_pairs={{0,8},{1,9},{2,10},{3,11},{4,12},{5,13},{6,14},{7,15},{8,0},{9,1},... | collective-permute-start | bytes 41480 | tf_op jit(solution)/shard_map/ppermute | solution.py:295
  101.8 4.1 %collective-permute-start.3 = (f32[3,1152]{1,0:T(4,128)S(1)}, f32[3,1152]{1,0:T(4,128)S(1)}, u32[]{:S(2)}, u32[]{:S(2)}) collective-permute-start(f32[3,1152]{1,0:T(4,128)S(1)} %add_add_fusion), channel_id=1, source_target_pairs={{0,4},{1,5},{2,6},{3,7},{4,0},{5,1},{6,2},{7,3},{8,12},{9,13},{10,... | collective-permute-start | bytes 41480 | tf_op jit(solution)/shard_map/ppermute | solution.py:295

commit v7 on v6

--- a/solution.py
+++ b/solution.py
@@ -106,6 +106,7 @@
         refs = refs[2:]
     key_rows, value_rows, key_cols, value_cols, key_grad, value_grad, near_flat, sem = refs
     step = pl.program_id(0)
+    single = not split and group == items.shape[0]
     load = pltpu.make_async_copy(weight, held, sem)
     chunks = items.shape[0]
     key_chunks = key_rows.shape[0] // LANES
@@ -129,8 +130,9 @@
             value_rows[at, :] = jnp.concatenate(
                 [values, jnp.ones((pad, LANES), F32)], axis=0
             ).T.astype(BF16)
-        key_grad[...] = jnp.zeros_like(key_grad)
-        value_grad[...] = jnp.zeros_like(value_grad)
+        if not single:
+            key_grad[...] = jnp.zeros_like(key_grad)
+            value_grad[...] = jnp.zeros_like(value_grad)
 
     block = [items[step * group + g].astype(F32) for g in range(group)]
     queries = jnp.concatenate([b[:head_size] for b in block], axis=1)
@@ -158,8 +160,18 @@
     )
     score_grad = (weights.astype(F32) * centred_grad * att_scale).astype(BF16)
     query_grad = jnp.dot(key_cols[...], score_grad, preferred_element_type=F32)
-    key_grad[...] += jnp.dot(score_grad, queries.T.astype(BF16), preferred_element_type=F32)
-    value_grad[...] += jnp.dot(weights, grads.T.astype(BF16), preferred_element_type=F32)
+    keys_of = jnp.dot(score_grad, queries.T.astype(BF16), preferred_element_type=F32)
+    values_of = jnp.dot(weights, grads.T.astype(BF16), preferred_element_type=F32)
+    if single:
+        for s in range(key_chunks):
+            at = slice(s * LANES, (s + 1) * LANES)
+            near[s] = jnp.concatenate(
+                [attended[:, at], query_grad[:, at], keys_of[at, :].T, values_of[at, :].T], axis=0
+            ).astype(BF16)
+        load.wait()
+        return
+    key_grad[...] += keys_of
+    value_grad[...] += values_of
     for g in range(group):
         at = slice(g * LANES, (g + 1) * LANES)
         near_flat[step * group + g] = jnp.concatenate(
@@ -227,13 +239,16 @@
 ):
     width = tokens.shape[1]
     flat = [items[head].astype(F32) for head in range(H)]
+    back = jnp.zeros((width, tokens.shape[0]), F32)
     for part in range(3):
-        grad_cols[part * width : (part + 1) * width, :] = jnp.concatenate(
+        at = slice(part * width, (part + 1) * width)
+        grad_cols[at, :] = jnp.concatenate(
             [x[(part + 1) * head_size : (part + 2) * head_size] for x in flat], axis=0
         ).astype(BF16)
+        back = back + jnp.dot(qkv_w[:, at], grad_cols[at, :], preferred_element_type=F32)
+    back = back.T
     att = jnp.concatenate([x[:head_size] for x in flat], axis=0).T.astype(BF16)
     out = jnp.dot(att, out_w[...], preferred_element_type=F32)
-    back = jnp.dot(qkv_w[...], grad_cols[...], preferred_element_type=F32).T
     _, normed, _ = normalise(tokens[...])
     branch[...] = out
     mod_grad[...] = back

time: 107 us -> 106 us (level)
  no operation moved by 1% of the time
where the time goes in v7:
time: 106 us
  blocking collectives  69.6 us (66%)
  Pallas kernels  25.6 us (24%)
  starting transfers between devices  6.47 us (6%)
  waiting for transfers between devices  3.19 us (3%)
    all_to_all x2, blocking collectives, exchange(): lax.all_to_all(blocks, 'seq', split_axis=0, concat_axis=0, tiled=True)  69.6 us
    pallas_call x1, Pallas kernels, attend(): pl.pallas_call(functools.partial(attend_kernel, head_size, group, split),...  14.7 us
    pallas_call x1, Pallas kernels, project(): pl.pallas_call(functools.partial(project_kernel, head_size), in_specs=[hb...  6.88 us
    ppermute x6, starting transfers between devices, from_partner(): lax.ppermute(shard, axis, [(i, i ^ stride) for i in range(lax.axis_size(a...  6.47 us
    ppermute x6, waiting for transfers between devices, from_partner(): lax.ppermute(shard, axis, [(i, i ^ stride) for i in range(lax.axis_size(a...  3.19 us
    pallas_call x1, Pallas kernels, gather(): pl.pallas_call(functools.partial(gather_kernel, width // H), in_specs=[vm...  2.94 us
  transfers between devices with their start and end apart: 6, of which 4 were waited for; matrix products, arithmetic and copies ran while one was open for 0% of the time, Pallas kernels for 1%

profile of v7, /device:TPU:0, one launch (start us, length us, event | category | flops | bytes accessed | tf_op | source)
XLA Modules:
  0.0 106.3 jit_solution(3380506207699806243)
XLA Ops:
  0.6 6.9 %project.1 = bf16[16,288,128]{2,1,0:T(8,128)(2,1)} custom-call(bf16[128,1152]{1,0:T(8,128)(2,1)} %tokens.3, f32[1152]{0:T(1024)} %refs_1_.1, f32[1152]{0:T(1024)} %scale.1, f32[1152]{0:T(1024)} %gate.1, bf16[128,1152]{1,0:T(8,128)(2,1)} %cot.3, bf16[1152,1152]{1,0:T(8,128)(2,1)} %out_w.1, bf16[1152,3456]{1,0:T(8,128)(2,1)} %weight.1), custom_call_target="tpu_custom_call" | custom-call | tf_op jit(solution)/shard_map/project/pallas_call | solution.py:88
  7.5 36.9 %all_to_all.10.items = bf16[16,288,128]{2,1,0:T(8,128)(2,1)S(1)} all-to-all(bf16[16,288,128]{2,1,0:T(8,128)(2,1)} %project.1), channel_id=1, replica_groups=mesh['groups'=2,'seq'=16] {'seq'}, dimensions={0} | all-to-all | bytes 2359296 | tf_op jit(solution)/shard_map/all_to_all | solution.py:314
  44.4 14.7 %attend.1 = (bf16[1152,3456]{1,0:T(8,128)(2,1)S(1)}, bf16[16,288,128]{2,1,0:T(8,128)(2,1)S(1)}) custom-call(bf16[16,288,128]{2,1,0:T(8,128)(2,1)S(1)} %all_to_all.10.items, bf16[1152,3456]{1,0:T(8,128)(2,1)} %weight.1), custom_call_target="tpu_custom_call" | custom-call | tf_op jit(solution)/shard_map/attend/pallas_call | solution.py:216
  59.1 0.0 copy-start.1
  59.1 0.0 copy-start.2
  59.1 32.7 %all_to_all.11.items = bf16[16,288,128]{2,1,0:T(8,128)(2,1)S(1)} all-to-all(bf16[16,288,128]{2,1,0:T(8,128)(2,1)S(1)} %get-tuple-element.10), channel_id=1, replica_groups=mesh['groups'=2,'seq'=16] {'seq'}, dimensions={0} | all-to-all | bytes 2359296 | tf_op jit(solution)/shard_map/all_to_all | solution.py:314
  91.8 0.0 copy-start.3
  91.8 0.0 copy-start.4
  91.9 2.9 %gather.1 = (f32[128,1152]{1,0:T(8,128)S(1)}, f32[128,1152]{1,0:T(8,128)S(1)}, f32[3,1152]{1,0:T(4,128)S(1)}) custom-call(bf16[16,288,128]{2,1,0:T(8,128)(2,1)S(1)} %all_to_all.11.items, bf16[128,1152]{1,0:T(8,128)(2,1)S(1)} %copy-done.1, bf16[1152,3456]{1,0:T(8,128)(2,1)S(1)} %get-tuple-element.11.qkv_w, bf16[1152,1152]{1,0:T(8,128)(2,1)S(1)} %copy-done, ...), custom_call_target="tpu_custom_call" | custom-call | tf_op jit(solution)/shard_map/gather/pallas_call | solution.py:268
  94.8 0.6 collective-permute-start.2
  95.4 1.4 %collective-permute-start.1 = (f32[3,1152]{1,0:T(4,128)S(1)}, f32[3,1152]{1,0:T(4,128)S(1)}, u32[]{:S(2)}, u32[]{:S(2)}) collective-permute-start(f32[3,1152]{1,0:T(4,128)S(1)} %get-tuple-element.16), channel_id=1, source_target_pairs={{0,2},{1,3},{2,0},{3,1},{4,6},{5,7},{6,4},{7,5},{8,10},{9,11},{10,... | collective-permute-start | bytes 41480 | tf_op jit(solution)/shard_map/ppermute | solution.py:310
  96.8 0.0 collective-permute-start
  96.8 1.2 %collective-permute-done.2 = f32[3,1152]{1,0:T(4,128)S(1)} collective-permute-done((f32[3,1152]{1,0:T(4,128)S(1)}, f32[3,1152]{1,0:T(4,128)S(1)}, u32[]{:S(2)}, u32[]{:S(2)}) %collective-permute-start.2) | collective-permute-done | bytes 13856 | tf_op jit(solution)/shard_map/ppermute | solution.py:310
  98.1 1.1 %collective-permute-done.1 = f32[3,1152]{1,0:T(4,128)S(1)} collective-permute-done((f32[3,1152]{1,0:T(4,128)S(1)}, f32[3,1152]{1,0:T(4,128)S(1)}, u32[]{:S(2)}, u32[]{:S(2)}) %collective-permute-start.1) | collective-permute-done | bytes 13856 | tf_op jit(solution)/shard_map/ppermute | solution.py:310
  99.2 0.0 collective-permute-done
  99.2 1.7 %collective-permute-start.5 = (f32[3,1152]{1,0:T(4,128)S(1)}, f32[3,1152]{1,0:T(4,128)S(1)}, u32[]{:S(2)}, u32[]{:S(2)}) collective-permute-start(f32[3,1152]{1,0:T(4,128)S(1)} %add_add_fusion), channel_id=1, source_target_pairs={{0,12},{1,13},{2,14},{3,15},{4,8},{5,9},{6,10},{7,11},{8,4},{9,5},... | collective-permute-start | bytes 41480 | tf_op jit(solution)/shard_map/ppermute | solution.py:310
  101.0 0.5 collective-permute-start.4
  101.5 2.2 %collective-permute-start.3 = (f32[3,1152]{1,0:T(4,128)S(1)}, f32[3,1152]{1,0:T(4,128)S(1)}, u32[]{:S(2)}, u32[]{:S(2)}) collective-permute-start(f32[3,1152]{1,0:T(4,128)S(1)} %add_add_fusion), channel_id=1, source_target_pairs={{0,4},{1,5},{2,6},{3,7},{4,0},{5,1},{6,2},{7,3},{8,12},{9,13},{10,... | collective-permute-start | bytes 41480 | tf_op jit(solution)/shard_map/ppermute | solution.py:310
  103.7 0.0 copy-done.3
  103.7 1.1 %finish.1 = (bf16[128,1152]{1,0:T(8,128)(2,1)}, bf16[128,1152]{1,0:T(8,128)(2,1)}) custom-call(f32[128,1152]{1,0:T(8,128)S(1)} %get-tuple-element.12.branch, f32[128,1152]{1,0:T(8,128)S(1)} %get-tuple-element.13.mod_grad, bf16[128,1152]{1,0:T(8,128)(2,1)S(1)} %copy-done.1, f32[1152]{0:T(1024)S(1)} %copy-done.3, f32[1152]{0:T(1024)S(1)} %copy-done.4, ...), custom_call_target="tpu_custom_call" | custom-call | flops 4423680 | bytes 2359296 | tf_op jit(solution)/shard_map/finish/pallas_call | solution.py:296
  104.8 0.1 collective-permute-done.5
  105.0 0.7 collective-permute-done.4
  105.6 0.0 collective-permute-done.3
  105.6 0.6 add_multiply_fusion
  (6 shorter events, 0.0 us)
Async XLA Ops:
  44.4 47.4 %copy-start = (bf16[1152,1152]{1,0:T(8,128)(2,1)S(1)}, bf16[1152,1152]{1,0:T(8,128)(2,1)}, u32[]{:S(2)}) copy-start(bf16[1152,1152]{1,0:T(8,128)(2,1)} %out_w.1) | copy-start | bytes 7962628
  59.1 32.7 %copy-start.1 = (bf16[128,1152]{1,0:T(8,128)(2,1)S(1)}, bf16[128,1152]{1,0:T(8,128)(2,1)}, u32[]{:S(2)}) copy-start(bf16[128,1152]{1,0:T(8,128)(2,1)} %tokens.3) | copy-start | bytes 884740
  59.1 32.7 %copy-start.2 = (bf16[128,1152]{1,0:T(8,128)(2,1)S(1)}, bf16[128,1152]{1,0:T(8,128)(2,1)}, u32[]{:S(2)}) copy-start(bf16[128,1152]{1,0:T(8,128)(2,1)} %cot.3) | copy-start | bytes 884740
  91.8 11.8 %copy-start.3 = (f32[1152]{0:T(1024)S(1)}, f32[1152]{0:T(1024)}, u32[]{:S(2)}) copy-start(f32[1152]{0:T(1024)} %scale.1) | copy-start | bytes 13828
  91.8 11.8 %copy-start.4 = (f32[1152]{0:T(1024)S(1)}, f32[1152]{0:T(1024)}, u32[]{:S(2)}) copy-start(f32[1152]{0:T(1024)} %gate.1) | copy-start | bytes 13828
  94.8 3.3 %collective-permute-start.2 = (f32[3,1152]{1,0:T(4,128)S(1)}, f32[3,1152]{1,0:T(4,128)S(1)}, u32[]{:S(2)}, u32[]{:S(2)}) collective-permute-start(f32[3,1152]{1,0:T(4,128)S(1)} %get-tuple-element.16), channel_id=1, source_target_pairs={{0,3},{1,2},{2,1},{3,0},{4,7},{5,6},{6,5},{7,4},{8,11},{9,10},{10,... | collective-permute-start | bytes 41480 | tf_op jit(solution)/shard_map/ppermute | solution.py:310
  95.4 3.8 %collective-permute-start.1 = (f32[3,1152]{1,0:T(4,128)S(1)}, f32[3,1152]{1,0:T(4,128)S(1)}, u32[]{:S(2)}, u32[]{:S(2)}) collective-permute-start(f32[3,1152]{1,0:T(4,128)S(1)} %get-tuple-element.16), channel_id=1, source_target_pairs={{0,2},{1,3},{2,0},{3,1},{4,6},{5,7},{6,4},{7,5},{8,10},{9,11},{10,... | collective-permute-start | bytes 41480 | tf_op jit(solution)/shard_map/ppermute | solution.py:310
  96.8 2.4 %collective-permute-start = (f32[3,1152]{1,0:T(4,128)S(1)}, f32[3,1152]{1,0:T(4,128)S(1)}, u32[]{:S(2)}, u32[]{:S(2)}) collective-permute-start(f32[3,1152]{1,0:T(4,128)S(1)} %get-tuple-element.16), channel_id=1, source_target_pairs={{0,1},{1,0},{2,3},{3,2},{4,5},{5,4},{6,7},{7,6},{8,9},{9,8},{10,11... | collective-permute-start | bytes 41480 | tf_op jit(solution)/shard_map/ppermute | solution.py:310
  99.2 5.7 %collective-permute-start.5 = (f32[3,1152]{1,0:T(4,128)S(1)}, f32[3,1152]{1,0:T(4,128)S(1)}, u32[]{:S(2)}, u32[]{:S(2)}) collective-permute-start(f32[3,1152]{1,0:T(4,128)S(1)} %add_add_fusion), channel_id=1, source_target_pairs={{0,12},{1,13},{2,14},{3,15},{4,8},{5,9},{6,10},{7,11},{8,4},{9,5},... | collective-permute-start | bytes 41480 | tf_op jit(solution)/shard_map/ppermute | solution.py:310
  101.0 4.7 %collective-permute-start.4 = (f32[3,1152]{1,0:T(4,128)S(1)}, f32[3,1152]{1,0:T(4,128)S(1)}, u32[]{:S(2)}, u32[]{:S(2)}) collective-permute-start(f32[3,1152]{1,0:T(4,128)S(1)} %add_add_fusion), channel_id=1, source_target_pairs={{0,8},{1,9},{2,10},{3,11},{4,12},{5,13},{6,14},{7,15},{8,0},{9,1},... | collective-permute-start | bytes 41480 | tf_op jit(solution)/shard_map/ppermute | solution.py:310
  101.5 4.1 %collective-permute-start.3 = (f32[3,1152]{1,0:T(4,128)S(1)}, f32[3,1152]{1,0:T(4,128)S(1)}, u32[]{:S(2)}, u32[]{:S(2)}) collective-permute-start(f32[3,1152]{1,0:T(4,128)S(1)} %add_add_fusion), channel_id=1, source_target_pairs={{0,4},{1,5},{2,6},{3,7},{4,0},{5,1},{6,2},{7,3},{8,12},{9,13},{10,... | collective-permute-start | bytes 41480 | tf_op jit(solution)/shard_map/ppermute | solution.py:310

commit v8 on v7

--- a/solution.py
+++ b/solution.py
@@ -48,17 +48,21 @@
         pltpu.make_async_copy(sources[6].at[:, at], qkv_w.at[:, at], sems.at[6 + part])
         for part, at in enumerate(parts)
     ]
-    for copy in copies:
+    for copy in copies[:5] + copies[6:] + copies[5:6]:
         copy.start()
-    for copy in copies[:5]:
+    for copy in copies[:3]:
         copy.wait()
     _, normed, _ = normalise(tokens[...])
     modulated = (normed * (1.0 + row(scale)) + row(shift)).astype(BF16)
-    gated = (row(gate) * cot[...].astype(F32)).astype(BF16)
-    copies[5].wait()
-    pulled = lax.dot_general(
-        out_w[...], gated, (((1,), (1,)), ((), ())), preferred_element_type=F32
-    )
+
+    def pulled_of():
+        copies[3].wait()
+        copies[4].wait()
+        gated = (row(gate) * cot[...].astype(F32)).astype(BF16)
+        copies[5].wait()
+        return lax.dot_general(
+            out_w[...], gated, (((1,), (1,)), ((), ())), preferred_element_type=F32
+        )
 
     def part_of(part):
         copies[6 + part].wait()
@@ -74,7 +78,7 @@
         return copy
 
     leaving = [send(part_of(0), part_of(1), 0)]
-    leaving.append(send(part_of(2), pulled, 1))
+    leaving.append(send(part_of(2), pulled_of(), 1))
     for copy in leaving:
         copy.wait()
 

time: 106 us -> 106 us (level)
  no operation moved by 1% of the time
where the time goes in v8:
time: 106 us
  blocking collectives  69.6 us (66%)
  Pallas kernels  25 us (24%)
  starting transfers between devices  6.47 us (6%)
  waiting for transfers between devices  3.19 us (3%)
    all_to_all x2, blocking collectives, exchange(): lax.all_to_all(blocks, 'seq', split_axis=0, concat_axis=0, tiled=True)  69.6 us
    pallas_call x1, Pallas kernels, attend(): pl.pallas_call(functools.partial(attend_kernel, head_size, group, split),...  14.7 us
    ppermute x6, starting transfers between devices, from_partner(): lax.ppermute(shard, axis, [(i, i ^ stride) for i in range(lax.axis_size(a...  6.47 us
    pallas_call x1, Pallas kernels, project(): pl.pallas_call(functools.partial(project_kernel, head_size), in_specs=[hb...  6.21 us
    ppermute x6, waiting for transfers between devices, from_partner(): lax.ppermute(shard, axis, [(i, i ^ stride) for i in range(lax.axis_size(a...  3.19 us
    pallas_call x1, Pallas kernels, gather(): pl.pallas_call(functools.partial(gather_kernel, width // H), in_specs=[vm...  2.94 us
  transfers between devices with their start and end apart: 6, of which 4 were waited for; matrix products, arithmetic and copies ran while one was open for 0% of the time, Pallas kernels for 1%

profile of v8, /device:TPU:0, one launch (start us, length us, event | category | flops | bytes accessed | tf_op | source)
XLA Modules:
  0.0 105.6 jit_solution(2787421912444280384)
XLA Ops:
  0.6 6.2 %project.1 = bf16[16,288,128]{2,1,0:T(8,128)(2,1)} custom-call(bf16[128,1152]{1,0:T(8,128)(2,1)} %tokens.3, f32[1152]{0:T(1024)} %refs_1_.1, f32[1152]{0:T(1024)} %scale.1, f32[1152]{0:T(1024)} %gate.1, bf16[128,1152]{1,0:T(8,128)(2,1)} %cot.3, bf16[1152,1152]{1,0:T(8,128)(2,1)} %out_w.1, bf16[1152,3456]{1,0:T(8,128)(2,1)} %weight.1), custom_call_target="tpu_custom_call" | custom-call | tf_op jit(solution)/shard_map/project/pallas_call | solution.py:92
  6.8 36.9 %all_to_all.10.items = bf16[16,288,128]{2,1,0:T(8,128)(2,1)S(1)} all-to-all(bf16[16,288,128]{2,1,0:T(8,128)(2,1)} %project.1), channel_id=1, replica_groups=mesh['groups'=2,'seq'=16] {'seq'}, dimensions={0} | all-to-all | bytes 2359296 | tf_op jit(solution)/shard_map/all_to_all | solution.py:318
  43.7 14.7 %attend.1 = (bf16[1152,3456]{1,0:T(8,128)(2,1)S(1)}, bf16[16,288,128]{2,1,0:T(8,128)(2,1)S(1)}) custom-call(bf16[16,288,128]{2,1,0:T(8,128)(2,1)S(1)} %all_to_all.10.items, bf16[1152,3456]{1,0:T(8,128)(2,1)} %weight.1), custom_call_target="tpu_custom_call" | custom-call | tf_op jit(solution)/shard_map/attend/pallas_call | solution.py:220
  58.4 0.0 copy-start.1
  58.4 0.0 copy-start.2
  58.4 32.7 %all_to_all.11.items = bf16[16,288,128]{2,1,0:T(8,128)(2,1)S(1)} all-to-all(bf16[16,288,128]{2,1,0:T(8,128)(2,1)S(1)} %get-tuple-element.10), channel_id=1, replica_groups=mesh['groups'=2,'seq'=16] {'seq'}, dimensions={0} | all-to-all | bytes 2359296 | tf_op jit(solution)/shard_map/all_to_all | solution.py:318
  91.1 0.0 copy-done
  91.2 0.0 copy-start.3
  91.2 0.0 copy-start.4
  91.2 2.9 %gather.1 = (f32[128,1152]{1,0:T(8,128)S(1)}, f32[128,1152]{1,0:T(8,128)S(1)}, f32[3,1152]{1,0:T(4,128)S(1)}) custom-call(bf16[16,288,128]{2,1,0:T(8,128)(2,1)S(1)} %all_to_all.11.items, bf16[128,1152]{1,0:T(8,128)(2,1)S(1)} %copy-done.1, bf16[1152,3456]{1,0:T(8,128)(2,1)S(1)} %get-tuple-element.11.qkv_w, bf16[1152,1152]{1,0:T(8,128)(2,1)S(1)} %copy-done, ...), custom_call_target="tpu_custom_call" | custom-call | tf_op jit(solution)/shard_map/gather/pallas_call | solution.py:272
  94.1 0.6 collective-permute-start.2
  94.8 1.4 %collective-permute-start.1 = (f32[3,1152]{1,0:T(4,128)S(1)}, f32[3,1152]{1,0:T(4,128)S(1)}, u32[]{:S(2)}, u32[]{:S(2)}) collective-permute-start(f32[3,1152]{1,0:T(4,128)S(1)} %get-tuple-element.16), channel_id=1, source_target_pairs={{0,2},{1,3},{2,0},{3,1},{4,6},{5,7},{6,4},{7,5},{8,10},{9,11},{10,... | collective-permute-start | bytes 41480 | tf_op jit(solution)/shard_map/ppermute | solution.py:314
  96.1 0.0 collective-permute-start
  96.1 1.2 %collective-permute-done.2 = f32[3,1152]{1,0:T(4,128)S(1)} collective-permute-done((f32[3,1152]{1,0:T(4,128)S(1)}, f32[3,1152]{1,0:T(4,128)S(1)}, u32[]{:S(2)}, u32[]{:S(2)}) %collective-permute-start.2) | collective-permute-done | bytes 13856 | tf_op jit(solution)/shard_map/ppermute | solution.py:314
  97.4 1.1 %collective-permute-done.1 = f32[3,1152]{1,0:T(4,128)S(1)} collective-permute-done((f32[3,1152]{1,0:T(4,128)S(1)}, f32[3,1152]{1,0:T(4,128)S(1)}, u32[]{:S(2)}, u32[]{:S(2)}) %collective-permute-start.1) | collective-permute-done | bytes 13856 | tf_op jit(solution)/shard_map/ppermute | solution.py:314
  98.5 0.0 collective-permute-done
  98.5 1.7 %collective-permute-start.5 = (f32[3,1152]{1,0:T(4,128)S(1)}, f32[3,1152]{1,0:T(4,128)S(1)}, u32[]{:S(2)}, u32[]{:S(2)}) collective-permute-start(f32[3,1152]{1,0:T(4,128)S(1)} %add_add_fusion), channel_id=1, source_target_pairs={{0,12},{1,13},{2,14},{3,15},{4,8},{5,9},{6,10},{7,11},{8,4},{9,5},... | collective-permute-start | bytes 41480 | tf_op jit(solution)/shard_map/ppermute | solution.py:314
  100.3 0.5 collective-permute-start.4
  100.8 2.2 %collective-permute-start.3 = (f32[3,1152]{1,0:T(4,128)S(1)}, f32[3,1152]{1,0:T(4,128)S(1)}, u32[]{:S(2)}, u32[]{:S(2)}) collective-permute-start(f32[3,1152]{1,0:T(4,128)S(1)} %add_add_fusion), channel_id=1, source_target_pairs={{0,4},{1,5},{2,6},{3,7},{4,0},{5,1},{6,2},{7,3},{8,12},{9,13},{10,... | collective-permute-start | bytes 41480 | tf_op jit(solution)/shard_map/ppermute | solution.py:314
  103.0 1.1 %finish.1 = (bf16[128,1152]{1,0:T(8,128)(2,1)}, bf16[128,1152]{1,0:T(8,128)(2,1)}) custom-call(f32[128,1152]{1,0:T(8,128)S(1)} %get-tuple-element.12.branch, f32[128,1152]{1,0:T(8,128)S(1)} %get-tuple-element.13.mod_grad, bf16[128,1152]{1,0:T(8,128)(2,1)S(1)} %copy-done.1, f32[1152]{0:T(1024)S(1)} %copy-done.3, f32[1152]{0:T(1024)S(1)} %copy-done.4, ...), custom_call_target="tpu_custom_call" | custom-call | flops 4423680 | bytes 2359296 | tf_op jit(solution)/shard_map/finish/pallas_call | solution.py:300
  104.1 0.1 collective-permute-done.5
  104.3 0.7 collective-permute-done.4
  104.9 0.0 collective-permute-done.3
  104.9 0.6 add_multiply_fusion
  (6 shorter events, 0.0 us)
Async XLA Ops:
  43.7 47.4 %copy-start = (bf16[1152,1152]{1,0:T(8,128)(2,1)S(1)}, bf16[1152,1152]{1,0:T(8,128)(2,1)}, u32[]{:S(2)}) copy-start(bf16[1152,1152]{1,0:T(8,128)(2,1)} %out_w.1) | copy-start | bytes 7962628
  58.4 32.7 %copy-start.1 = (bf16[128,1152]{1,0:T(8,128)(2,1)S(1)}, bf16[128,1152]{1,0:T(8,128)(2,1)}, u32[]{:S(2)}) copy-start(bf16[128,1152]{1,0:T(8,128)(2,1)} %tokens.3) | copy-start | bytes 884740
  58.4 32.7 %copy-start.2 = (bf16[128,1152]{1,0:T(8,128)(2,1)S(1)}, bf16[128,1152]{1,0:T(8,128)(2,1)}, u32[]{:S(2)}) copy-start(bf16[128,1152]{1,0:T(8,128)(2,1)} %cot.3) | copy-start | bytes 884740
  91.2 11.8 %copy-start.3 = (f32[1152]{0:T(1024)S(1)}, f32[1152]{0:T(1024)}, u32[]{:S(2)}) copy-start(f32[1152]{0:T(1024)} %scale.1) | copy-start | bytes 13828
  91.2 11.8 %copy-start.4 = (f32[1152]{0:T(1024)S(1)}, f32[1152]{0:T(1024)}, u32[]{:S(2)}) copy-start(f32[1152]{0:T(1024)} %gate.1) | copy-start | bytes 13828
  94.1 3.3 %collective-permute-start.2 = (f32[3,1152]{1,0:T(4,128)S(1)}, f32[3,1152]{1,0:T(4,128)S(1)}, u32[]{:S(2)}, u32[]{:S(2)}) collective-permute-start(f32[3,1152]{1,0:T(4,128)S(1)} %get-tuple-element.16), channel_id=1, source_target_pairs={{0,3},{1,2},{2,1},{3,0},{4,7},{5,6},{6,5},{7,4},{8,11},{9,10},{10,... | collective-permute-start | bytes 41480 | tf_op jit(solution)/shard_map/ppermute | solution.py:314
  94.8 3.8 %collective-permute-start.1 = (f32[3,1152]{1,0:T(4,128)S(1)}, f32[3,1152]{1,0:T(4,128)S(1)}, u32[]{:S(2)}, u32[]{:S(2)}) collective-permute-start(f32[3,1152]{1,0:T(4,128)S(1)} %get-tuple-element.16), channel_id=1, source_target_pairs={{0,2},{1,3},{2,0},{3,1},{4,6},{5,7},{6,4},{7,5},{8,10},{9,11},{10,... | collective-permute-start | bytes 41480 | tf_op jit(solution)/shard_map/ppermute | solution.py:314
  96.1 2.4 %collective-permute-start = (f32[3,1152]{1,0:T(4,128)S(1)}, f32[3,1152]{1,0:T(4,128)S(1)}, u32[]{:S(2)}, u32[]{:S(2)}) collective-permute-start(f32[3,1152]{1,0:T(4,128)S(1)} %get-tuple-element.16), channel_id=1, source_target_pairs={{0,1},{1,0},{2,3},{3,2},{4,5},{5,4},{6,7},{7,6},{8,9},{9,8},{10,11... | collective-permute-start | bytes 41480 | tf_op jit(solution)/shard_map/ppermute | solution.py:314
  98.5 5.7 %collective-permute-start.5 = (f32[3,1152]{1,0:T(4,128)S(1)}, f32[3,1152]{1,0:T(4,128)S(1)}, u32[]{:S(2)}, u32[]{:S(2)}) collective-permute-start(f32[3,1152]{1,0:T(4,128)S(1)} %add_add_fusion), channel_id=1, source_target_pairs={{0,12},{1,13},{2,14},{3,15},{4,8},{5,9},{6,10},{7,11},{8,4},{9,5},... | collective-permute-start | bytes 41480 | tf_op jit(solution)/shard_map/ppermute | solution.py:314
  100.3 4.7 %collective-permute-start.4 = (f32[3,1152]{1,0:T(4,128)S(1)}, f32[3,1152]{1,0:T(4,128)S(1)}, u32[]{:S(2)}, u32[]{:S(2)}) collective-permute-start(f32[3,1152]{1,0:T(4,128)S(1)} %add_add_fusion), channel_id=1, source_target_pairs={{0,8},{1,9},{2,10},{3,11},{4,12},{5,13},{6,14},{7,15},{8,0},{9,1},... | collective-permute-start | bytes 41480 | tf_op jit(solution)/shard_map/ppermute | solution.py:314
  100.8 4.1 %collective-permute-start.3 = (f32[3,1152]{1,0:T(4,128)S(1)}, f32[3,1152]{1,0:T(4,128)S(1)}, u32[]{:S(2)}, u32[]{:S(2)}) collective-permute-start(f32[3,1152]{1,0:T(4,128)S(1)} %add_add_fusion), channel_id=1, source_target_pairs={{0,4},{1,5},{2,6},{3,7},{4,0},{5,1},{6,2},{7,3},{8,12},{9,13},{10,... | collective-permute-start | bytes 41480 | tf_op jit(solution)/shard_map/ppermute | solution.py:314

commit v9 on v8

--- a/solution.py
+++ b/solution.py
@@ -48,37 +48,48 @@
         pltpu.make_async_copy(sources[6].at[:, at], qkv_w.at[:, at], sems.at[6 + part])
         for part, at in enumerate(parts)
     ]
-    for copy in copies[:5] + copies[6:] + copies[5:6]:
+    middle = H // 2 * head_size
+    halves = [slice(0, middle), slice(middle, width)]
+    out_copies = [
+        pltpu.make_async_copy(sources[5].at[at, :], out_w.at[at, :], sems.at[sem])
+        for at, sem in zip(halves, (5, 11))
+    ]
+    for copy in copies[:5] + copies[6:] + out_copies:
         copy.start()
     for copy in copies[:3]:
         copy.wait()
     _, normed, _ = normalise(tokens[...])
     modulated = (normed * (1.0 + row(scale)) + row(shift)).astype(BF16)
 
-    def pulled_of():
-        copies[3].wait()
-        copies[4].wait()
-        gated = (row(gate) * cot[...].astype(F32)).astype(BF16)
-        copies[5].wait()
+    def pulled_of(i, gated):
+        out_copies[i].wait()
         return lax.dot_general(
-            out_w[...], gated, (((1,), (1,)), ((), ())), preferred_element_type=F32
+            out_w[halves[i], :], gated, (((1,), (1,)), ((), ())), preferred_element_type=F32
         )
 
     def part_of(part):
         copies[6 + part].wait()
         return jnp.dot(modulated, qkv_w[:, parts[part]], preferred_element_type=F32).T
 
-    def send(first, second, half):
+    def send(first, second, heads, half, sem):
         rows = slice(half * 2 * head_size, (half + 1) * 2 * head_size)
-        for head in range(H):
-            at = slice(head * head_size, (head + 1) * head_size)
+        for i, head in enumerate(heads):
+            at = slice(i * head_size, (i + 1) * head_size)
             packed[head, rows, :] = jnp.concatenate([first[at], second[at]], axis=0).astype(BF16)
-        copy = pltpu.make_async_copy(packed.at[:, rows, :], out.at[:, rows, :], sems.at[9 + half])
+        block = (slice(heads[0], heads[-1] + 1), rows)
+        copy = pltpu.make_async_copy(packed.at[block], out.at[block], sems.at[sem])
         copy.start()
         return copy
 
-    leaving = [send(part_of(0), part_of(1), 0)]
-    leaving.append(send(part_of(2), pulled_of(), 1))
+    leaving = [send(part_of(0), part_of(1), range(H), 0, 9)]
+    values = part_of(2)
+    copies[3].wait()
+    copies[4].wait()
+    gated = (row(gate) * cot[...].astype(F32)).astype(BF16)
+    lower = pulled_of(0, gated)
+    leaving.append(send(values[:middle], lower, range(H // 2), 1, 10))
+    upper = pulled_of(1, gated)
+    leaving.append(send(values[middle:], upper, range(H // 2, H), 1, 12))
     for copy in leaving:
         copy.wait()
 
@@ -95,7 +106,7 @@
         out_specs=hbm,
         out_shape=jax.ShapeDtypeStruct(packed, BF16),
         scratch_shapes=[pltpu.VMEM(x.shape, x.dtype) for x in operands]
-        + [pltpu.SemaphoreType.DMA((11,)), pltpu.VMEM(packed, BF16)],
+        + [pltpu.SemaphoreType.DMA((13,)), pltpu.VMEM(packed, BF16)],
         compiler_params=pltpu.CompilerParams(vmem_limit_bytes=PROJECT_LIMIT),
         name="project",
     )(*operands)

time: 106 us -> 106 us (level)
  no operation moved by 1% of the time
where the time goes in v9:
time: 106 us
  blocking collectives  69.6 us (66%)
  Pallas kernels  25.5 us (24%)
  starting transfers between devices  6.47 us (6%)
  waiting for transfers between devices  3.19 us (3%)
    all_to_all x2, blocking collectives, exchange(): lax.all_to_all(blocks, 'seq', split_axis=0, concat_axis=0, tiled=True)  69.6 us
    pallas_call x1, Pallas kernels, attend(): pl.pallas_call(functools.partial(attend_kernel, head_size, group, split),...  14.7 us
    pallas_call x1, Pallas kernels, project(): pl.pallas_call(functools.partial(project_kernel, head_size), in_specs=[hb...  6.73 us
    ppermute x6, starting transfers between devices, from_partner(): lax.ppermute(shard, axis, [(i, i ^ stride) for i in range(lax.axis_size(a...  6.47 us
    ppermute x6, waiting for transfers between devices, from_partner(): lax.ppermute(shard, axis, [(i, i ^ stride) for i in range(lax.axis_size(a...  3.19 us
    pallas_call x1, Pallas kernels, gather(): pl.pallas_call(functools.partial(gather_kernel, width // H), in_specs=[vm...  2.94 us
  transfers between devices with their start and end apart: 6, of which 4 were waited for; matrix products, arithmetic and copies ran while one was open for 0% of the time, Pallas kernels for 1%

profile of v9, /device:TPU:0, one launch (start us, length us, event | category | flops | bytes accessed | tf_op | source)
XLA Modules:
  0.0 106.1 jit_solution(8455932827249426341)
XLA Ops:
  0.6 6.7 %project.1 = bf16[16,288,128]{2,1,0:T(8,128)(2,1)} custom-call(bf16[128,1152]{1,0:T(8,128)(2,1)} %tokens.3, f32[1152]{0:T(1024)} %refs_1_.1, f32[1152]{0:T(1024)} %scale.1, f32[1152]{0:T(1024)} %gate.1, bf16[128,1152]{1,0:T(8,128)(2,1)} %cot.3, bf16[1152,1152]{1,0:T(8,128)(2,1)} %out_w.1, bf16[1152,3456]{1,0:T(8,128)(2,1)} %weight.1), custom_call_target="tpu_custom_call" | custom-call | tf_op jit(solution)/shard_map/project/pallas_call | solution.py:103
  7.4 36.9 %all_to_all.10.items = bf16[16,288,128]{2,1,0:T(8,128)(2,1)S(1)} all-to-all(bf16[16,288,128]{2,1,0:T(8,128)(2,1)} %project.1), channel_id=1, replica_groups=mesh['groups'=2,'seq'=16] {'seq'}, dimensions={0} | all-to-all | bytes 2359296 | tf_op jit(solution)/shard_map/all_to_all | solution.py:329
  44.2 14.7 %attend.1 = (bf16[1152,3456]{1,0:T(8,128)(2,1)S(1)}, bf16[16,288,128]{2,1,0:T(8,128)(2,1)S(1)}) custom-call(bf16[16,288,128]{2,1,0:T(8,128)(2,1)S(1)} %all_to_all.10.items, bf16[1152,3456]{1,0:T(8,128)(2,1)} %weight.1), custom_call_target="tpu_custom_call" | custom-call | tf_op jit(solution)/shard_map/attend/pallas_call | solution.py:231
  58.9 0.0 copy-start.1
  58.9 0.0 copy-start.2
  59.0 32.7 %all_to_all.11.items = bf16[16,288,128]{2,1,0:T(8,128)(2,1)S(1)} all-to-all(bf16[16,288,128]{2,1,0:T(8,128)(2,1)S(1)} %get-tuple-element.10), channel_id=1, replica_groups=mesh['groups'=2,'seq'=16] {'seq'}, dimensions={0} | all-to-all | bytes 2359296 | tf_op jit(solution)/shard_map/all_to_all | solution.py:329
  91.7 0.0 copy-done.1
  91.7 0.0 copy-start.3
  91.7 0.0 copy-start.4
  91.7 2.9 %gather.1 = (f32[128,1152]{1,0:T(8,128)S(1)}, f32[128,1152]{1,0:T(8,128)S(1)}, f32[3,1152]{1,0:T(4,128)S(1)}) custom-call(bf16[16,288,128]{2,1,0:T(8,128)(2,1)S(1)} %all_to_all.11.items, bf16[128,1152]{1,0:T(8,128)(2,1)S(1)} %copy-done.1, bf16[1152,3456]{1,0:T(8,128)(2,1)S(1)} %get-tuple-element.11.qkv_w, bf16[1152,1152]{1,0:T(8,128)(2,1)S(1)} %copy-done, ...), custom_call_target="tpu_custom_call" | custom-call | tf_op jit(solution)/shard_map/gather/pallas_call | solution.py:283
  94.6 0.6 collective-permute-start.2
  95.3 1.4 %collective-permute-start.1 = (f32[3,1152]{1,0:T(4,128)S(1)}, f32[3,1152]{1,0:T(4,128)S(1)}, u32[]{:S(2)}, u32[]{:S(2)}) collective-permute-start(f32[3,1152]{1,0:T(4,128)S(1)} %get-tuple-element.16), channel_id=1, source_target_pairs={{0,2},{1,3},{2,0},{3,1},{4,6},{5,7},{6,4},{7,5},{8,10},{9,11},{10,... | collective-permute-start | bytes 41480 | tf_op jit(solution)/shard_map/ppermute | solution.py:325
  96.7 0.0 collective-permute-start
  96.7 1.2 %collective-permute-done.2 = f32[3,1152]{1,0:T(4,128)S(1)} collective-permute-done((f32[3,1152]{1,0:T(4,128)S(1)}, f32[3,1152]{1,0:T(4,128)S(1)}, u32[]{:S(2)}, u32[]{:S(2)}) %collective-permute-start.2) | collective-permute-done | bytes 13856 | tf_op jit(solution)/shard_map/ppermute | solution.py:325
  97.9 1.1 %collective-permute-done.1 = f32[3,1152]{1,0:T(4,128)S(1)} collective-permute-done((f32[3,1152]{1,0:T(4,128)S(1)}, f32[3,1152]{1,0:T(4,128)S(1)}, u32[]{:S(2)}, u32[]{:S(2)}) %collective-permute-start.1) | collective-permute-done | bytes 13856 | tf_op jit(solution)/shard_map/ppermute | solution.py:325
  99.0 0.0 collective-permute-done
  99.1 1.7 %collective-permute-start.5 = (f32[3,1152]{1,0:T(4,128)S(1)}, f32[3,1152]{1,0:T(4,128)S(1)}, u32[]{:S(2)}, u32[]{:S(2)}) collective-permute-start(f32[3,1152]{1,0:T(4,128)S(1)} %add_add_fusion), channel_id=1, source_target_pairs={{0,12},{1,13},{2,14},{3,15},{4,8},{5,9},{6,10},{7,11},{8,4},{9,5},... | collective-permute-start | bytes 41480 | tf_op jit(solution)/shard_map/ppermute | solution.py:325
  100.8 0.5 collective-permute-start.4
  101.3 2.2 %collective-permute-start.3 = (f32[3,1152]{1,0:T(4,128)S(1)}, f32[3,1152]{1,0:T(4,128)S(1)}, u32[]{:S(2)}, u32[]{:S(2)}) collective-permute-start(f32[3,1152]{1,0:T(4,128)S(1)} %add_add_fusion), channel_id=1, source_target_pairs={{0,4},{1,5},{2,6},{3,7},{4,0},{5,1},{6,2},{7,3},{8,12},{9,13},{10,... | collective-permute-start | bytes 41480 | tf_op jit(solution)/shard_map/ppermute | solution.py:325
  103.5 1.1 %finish.1 = (bf16[128,1152]{1,0:T(8,128)(2,1)}, bf16[128,1152]{1,0:T(8,128)(2,1)}) custom-call(f32[128,1152]{1,0:T(8,128)S(1)} %get-tuple-element.12.branch, f32[128,1152]{1,0:T(8,128)S(1)} %get-tuple-element.13.mod_grad, bf16[128,1152]{1,0:T(8,128)(2,1)S(1)} %copy-done.1, f32[1152]{0:T(1024)S(1)} %copy-done.3, f32[1152]{0:T(1024)S(1)} %copy-done.4, ...), custom_call_target="tpu_custom_call" | custom-call | flops 4423680 | bytes 2359296 | tf_op jit(solution)/shard_map/finish/pallas_call | solution.py:311
  104.7 0.1 collective-permute-done.5
  104.8 0.7 collective-permute-done.4
  105.5 0.0 collective-permute-done.3
  105.5 0.6 add_multiply_fusion
  (6 shorter events, 0.0 us)
Async XLA Ops:
  44.2 47.4 %copy-start = (bf16[1152,1152]{1,0:T(8,128)(2,1)S(1)}, bf16[1152,1152]{1,0:T(8,128)(2,1)}, u32[]{:S(2)}) copy-start(bf16[1152,1152]{1,0:T(8,128)(2,1)} %out_w.1) | copy-start | bytes 7962628
  58.9 32.7 %copy-start.1 = (bf16[128,1152]{1,0:T(8,128)(2,1)S(1)}, bf16[128,1152]{1,0:T(8,128)(2,1)}, u32[]{:S(2)}) copy-start(bf16[128,1152]{1,0:T(8,128)(2,1)} %tokens.3) | copy-start | bytes 884740
  58.9 32.7 %copy-start.2 = (bf16[128,1152]{1,0:T(8,128)(2,1)S(1)}, bf16[128,1152]{1,0:T(8,128)(2,1)}, u32[]{:S(2)}) copy-start(bf16[128,1152]{1,0:T(8,128)(2,1)} %cot.3) | copy-start | bytes 884740
  91.7 11.8 %copy-start.3 = (f32[1152]{0:T(1024)S(1)}, f32[1152]{0:T(1024)}, u32[]{:S(2)}) copy-start(f32[1152]{0:T(1024)} %scale.1) | copy-start | bytes 13828
  91.7 11.8 %copy-start.4 = (f32[1152]{0:T(1024)S(1)}, f32[1152]{0:T(1024)}, u32[]{:S(2)}) copy-start(f32[1152]{0:T(1024)} %gate.1) | copy-start | bytes 13828
  94.6 3.3 %collective-permute-start.2 = (f32[3,1152]{1,0:T(4,128)S(1)}, f32[3,1152]{1,0:T(4,128)S(1)}, u32[]{:S(2)}, u32[]{:S(2)}) collective-permute-start(f32[3,1152]{1,0:T(4,128)S(1)} %get-tuple-element.16), channel_id=1, source_target_pairs={{0,3},{1,2},{2,1},{3,0},{4,7},{5,6},{6,5},{7,4},{8,11},{9,10},{10,... | collective-permute-start | bytes 41480 | tf_op jit(solution)/shard_map/ppermute | solution.py:325
  95.3 3.8 %collective-permute-start.1 = (f32[3,1152]{1,0:T(4,128)S(1)}, f32[3,1152]{1,0:T(4,128)S(1)}, u32[]{:S(2)}, u32[]{:S(2)}) collective-permute-start(f32[3,1152]{1,0:T(4,128)S(1)} %get-tuple-element.16), channel_id=1, source_target_pairs={{0,2},{1,3},{2,0},{3,1},{4,6},{5,7},{6,4},{7,5},{8,10},{9,11},{10,... | collective-permute-start | bytes 41480 | tf_op jit(solution)/shard_map/ppermute | solution.py:325
  96.7 2.4 %collective-permute-start = (f32[3,1152]{1,0:T(4,128)S(1)}, f32[3,1152]{1,0:T(4,128)S(1)}, u32[]{:S(2)}, u32[]{:S(2)}) collective-permute-start(f32[3,1152]{1,0:T(4,128)S(1)} %get-tuple-element.16), channel_id=1, source_target_pairs={{0,1},{1,0},{2,3},{3,2},{4,5},{5,4},{6,7},{7,6},{8,9},{9,8},{10,11... | collective-permute-start | bytes 41480 | tf_op jit(solution)/shard_map/ppermute | solution.py:325
  99.1 5.7 %collective-permute-start.5 = (f32[3,1152]{1,0:T(4,128)S(1)}, f32[3,1152]{1,0:T(4,128)S(1)}, u32[]{:S(2)}, u32[]{:S(2)}) collective-permute-start(f32[3,1152]{1,0:T(4,128)S(1)} %add_add_fusion), channel_id=1, source_target_pairs={{0,12},{1,13},{2,14},{3,15},{4,8},{5,9},{6,10},{7,11},{8,4},{9,5},... | collective-permute-start | bytes 41480 | tf_op jit(solution)/shard_map/ppermute | solution.py:325
  100.8 4.7 %collective-permute-start.4 = (f32[3,1152]{1,0:T(4,128)S(1)}, f32[3,1152]{1,0:T(4,128)S(1)}, u32[]{:S(2)}, u32[]{:S(2)}) collective-permute-start(f32[3,1152]{1,0:T(4,128)S(1)} %add_add_fusion), channel_id=1, source_target_pairs={{0,8},{1,9},{2,10},{3,11},{4,12},{5,13},{6,14},{7,15},{8,0},{9,1},... | collective-permute-start | bytes 41480 | tf_op jit(solution)/shard_map/ppermute | solution.py:325
  101.3 4.1 %collective-permute-start.3 = (f32[3,1152]{1,0:T(4,128)S(1)}, f32[3,1152]{1,0:T(4,128)S(1)}, u32[]{:S(2)}, u32[]{:S(2)}) collective-permute-start(f32[3,1152]{1,0:T(4,128)S(1)} %add_add_fusion), channel_id=1, source_target_pairs={{0,4},{1,5},{2,6},{3,7},{4,0},{5,1},{6,2},{7,3},{8,12},{9,13},{10,... | collective-permute-start | bytes 41480 | tf_op jit(solution)/shard_map/ppermute | solution.py:325
